TPU v7x, 32 devices: a whole 2x2x4 slice. The times are simulated.
32 devices in a mesh: blk: 16 (over z, y, core), rep: 2 (over x).
Axes of the slice: x: 2, y: 2, z: 4, core: 2. Of those that a mesh axis runs over, the one named last changes fastest.
Arguments:
- features: bfloat16 [16384, 256], P('blk'), may hold values from -6 to 6
- weight_self: bfloat16 [256, 256], replicated, may hold values from -0.375 to 0.375
- weight_neighbor: bfloat16 [256, 256], replicated, may hold values from -0.375 to 0.375
- bias_vector: float32 [256], replicated, may hold values from -3 to 3
- tile_row: int32 [16, 16, 64], P('blk', 'rep'), may hold values from 0 to 7
- tile_column: int32 [16, 16, 64], P('blk', 'rep'), may hold values from 0 to 7
- tile_value: int32 [16, 16, 64], P('blk', 'rep'), may hold values from 0 to 127
- tile_count: int32 [16, 16], P('blk', 'rep'), may hold values from 16 to 64
- tile_table: bfloat16 [4096, 128, 128], P(('blk', 'rep')), may hold values from -0.0625 to 0.0625
- cotangent: bfloat16 [16384, 256], P('blk'), may hold values from -6 to 6
Outputs:
- activations: bfloat16 [16384, 256], P('blk')
- grad_features: bfloat16 [16384, 256], P('blk')
- grad_weight_self: float32 [256, 256], replicated
- grad_weight_neighbor: float32 [256, 256], replicated
- grad_bias: float32 [256], replicated
All inputs are finite; a program needn't handle non-finite values.
Results may differ from a plain program's by a relative error of at most 0.025.
Values may be sent and summed in bfloat16 or wider, within the bound.
A program may use at most 64 MiB of HBM per device.

v0:
```python
import jax
import jax.numpy as jnp
from jax import lax
from jax.sharding import PartitionSpec as P


def from_behind(array, axis, by):
    length = lax.axis_size(axis)
    return lax.ppermute(array, axis, [(i, (i + by) % length) for i in range(length)])


def gather_terms(tile_table, source_blocks, row_pick, column_pick, value_pick, live_count, forward):
    slot_count = row_pick.shape[0]
    block_count = source_blocks.shape[0]
    is_live = jnp.arange(slot_count) < live_count
    tile_values = jnp.take(tile_table, value_pick, axis=0)
    if forward:
        picked = jnp.take(source_blocks, column_pick, axis=0)
        products = jnp.einsum(
            "kab,kbf->kaf", tile_values, picked, preferred_element_type=jnp.float32
        )
        target_pick = row_pick
    else:
        picked = jnp.take(source_blocks, row_pick, axis=0)
        products = jnp.einsum(
            "kab,kaf->kbf", tile_values, picked, preferred_element_type=jnp.float32
        )
        target_pick = column_pick
    placing = (
        (target_pick[:, None] == jnp.arange(block_count)[None, :]) & is_live[:, None]
    ).astype(jnp.float32)
    return jnp.einsum("kr,kaf->raf", placing, products, preferred_element_type=jnp.float32)


def on_device(
    features,
    weight_self,
    weight_neighbor,
    bias_vector,
    tile_row,
    tile_column,
    tile_value,
    tile_count,
    tile_table,
    cotangent,
):
    cycle_length = lax.axis_size("blk")
    replicas = lax.axis_size("rep")
    step_count = cycle_length // replicas
    rep_bits = replicas.bit_length() - 1
    replica = lax.axis_index("rep")
    row_total, feature_width = features.shape
    tile_size = tile_table.shape[1]
    block_count = row_total // tile_size
    row_lists = tile_row[0]
    column_lists = tile_column[0]
    value_lists = tile_value[0]
    live_counts = tile_count[0]

    def step_term(source_blocks, offset, forward):
        return gather_terms(
            tile_table,
            source_blocks,
            lax.dynamic_index_in_dim(row_lists, offset, 0, False),
            lax.dynamic_index_in_dim(column_lists, offset, 0, False),
            lax.dynamic_index_in_dim(value_lists, offset, 0, False),
            lax.dynamic_index_in_dim(live_counts, offset, 0, False),
            forward,
        )

    def shape_blocks(matrix):
        return matrix.reshape(block_count, tile_size, feature_width)

    feature_panel = features
    for bit_index in range(rep_bits):
        shifted = from_behind(feature_panel, "blk", step_count << bit_index)
        feature_panel = jnp.where(replica // (1 << bit_index) % 2 == 1, shifted, feature_panel)
    partial_sum = step_term(shape_blocks(feature_panel), 0, True)

    def cycle_step(offset, carry):
        panel_now, running = carry
        panel_now = from_behind(panel_now, "blk", 1)
        return (panel_now, running + step_term(shape_blocks(panel_now), offset, True))

    feature_panel, partial_sum = lax.fori_loop(
        1, step_count, cycle_step, (feature_panel, partial_sum)
    )
    partial_sum = partial_sum.reshape(row_total, feature_width)
    aggregate = lax.psum(partial_sum, "rep")
    aggregate_b = aggregate.astype(jnp.bfloat16)
    before = jnp.dot(features, weight_self, preferred_element_type=jnp.float32)
    before = (
        before
        + jnp.dot(aggregate_b, weight_neighbor, preferred_element_type=jnp.float32)
        + bias_vector
    )
    sigmoid_pre = jax.nn.sigmoid(before)
    output_rows = (before * sigmoid_pre).astype(jnp.bfloat16)
    derivative = sigmoid_pre * (1.0 + before * (1.0 - sigmoid_pre))
    grad_pre = (cotangent.astype(jnp.float32) * derivative).astype(jnp.bfloat16)
    contract_rows = (((0,), (0,)), ((), ()))
    contract_columns = (((1,), (1,)), ((), ()))
    grad_self = lax.dot_general(
        features, grad_pre, contract_rows, preferred_element_type=jnp.float32
    )
    grad_neighbor = lax.dot_general(
        aggregate_b, grad_pre, contract_rows, preferred_element_type=jnp.float32
    )
    grad_offset = jnp.sum(grad_pre.astype(jnp.float32), axis=0)
    self_term = lax.dot_general(
        grad_pre, weight_self, contract_columns, preferred_element_type=jnp.float32
    )
    sent_back = lax.dot_general(
        grad_pre, weight_neighbor, contract_columns, preferred_element_type=jnp.float32
    ).astype(jnp.bfloat16)
    grad_self, grad_neighbor, grad_offset = (
        lax.psum(grad_self.astype(jnp.bfloat16), "blk").astype(jnp.float32),
        lax.psum(grad_neighbor.astype(jnp.bfloat16), "blk").astype(jnp.float32),
        lax.psum(grad_offset.astype(jnp.bfloat16), "blk").astype(jnp.float32),
    )
    back_blocks = shape_blocks(sent_back)
    pushed = step_term(back_blocks, step_count - 1, False)

    def push_step(offset, running):
        running = from_behind(running, "blk", -1)
        return running + step_term(back_blocks, step_count - 1 - offset, False)

    pushed = lax.fori_loop(1, step_count, push_step, pushed)
    for bit_index in range(rep_bits):
        shifted = from_behind(
            pushed.astype(jnp.bfloat16), "blk", -(step_count << bit_index)
        ).astype(pushed.dtype)
        pushed = jnp.where(replica // (1 << bit_index) % 2 == 1, shifted, pushed)
    pushed = pushed.reshape(row_total, feature_width)
    neighbor_term = lax.psum(pushed.astype(jnp.bfloat16), "rep").astype(jnp.float32)
    grad_features = (self_term + neighbor_term).astype(jnp.bfloat16)
    return (output_rows, grad_features, grad_self, grad_neighbor, grad_offset)


def solution(mesh):
    placed = (
        P("blk", None),
        P(),
        P(),
        P(),
        P("blk", "rep", None),
        P("blk", "rep", None),
        P("blk", "rep", None),
        P("blk", "rep"),
        P(("blk", "rep"), None, None),
        P("blk", None),
    )
    return jax.shard_map(
        on_device,
        mesh=mesh,
        in_specs=placed,
        out_specs=(P("blk", None), P("blk", None), P(), P(), P()),
        check_vma=False,
    )
```

profile of v0, /device:TPU:0, one launch (start us, length us, event | category | flops | bytes accessed | tf_op | source)
XLA Modules:
  0.0 519.6 jit_solution(10854658101296210277)
XLA Ops:
  7.2 4.1 collective-permute-start.2
  19.4 4.4 gather_fusion.6
  25.8 9.0 %collective-permute-done.2 = bf16[1024,256]{1,0:T(8,128)(2,1)} collective-permute-done((bf16[1024,256]{1,0:T(8,128)(2,1)}, bf16[1024,256]{1,0:T(8,128)(2,1)}, u32[]{:S(2)}, u32[]{:S(2)}) %collective-permute-start.2) | collective-permute-done | bytes 524320 | tf_op jit(solution)/shard_map/ppermute | solution.py:9
  44.6 147.8 %while.32 = (s32[]{:T(128)}, bf16[1024,256]{1,0:T(8,128)(2,1)S(1)}, f32[8,128,256]{2,0,1:T(8,128)}, s32[8,64]{1,0:T(8,128)}, s32[8]{0:T(128)S(1)}, /*index=5*/s3...) while((s32[]{:T(128)}, bf16[1024,256]{1,0:T(8,128)(2,1)S(1)}, ...), condition=%wide.region_1.4_spmd, body=%wide.region_0.3_spmd.sunk | while | flops 573837120 | bytes 40906124 | solution.py:85
  50.4 5.5 %collective-permute-done = bf16[1024,256]{1,0:T(8,128)(2,1)S(1)} collective-permute-done((bf16[1024,256]{1,0:T(8,128)(2,1)S(1)}, bf16[1024,256]{1,0:T(8,128)(2,1)S(1)}, u32[]{:S(2)}, u32[]{:S(2)}) %collective-permute-start) | collective-permute-done | bytes 524320 | tf_op jit(solution)/shard_map/while/body/eval_jaxpr/ppermute | solution.py:9
  71.5 5.5 %collective-permute-done = bf16[1024,256]{1,0:T(8,128)(2,1)S(1)} collective-permute-done((bf16[1024,256]{1,0:T(8,128)(2,1)S(1)}, bf16[1024,256]{1,0:T(8,128)(2,1)S(1)}, u32[]{:S(2)}, u32[]{:S(2)}) %collective-permute-start) | collective-permute-done | bytes 524320 | tf_op jit(solution)/shard_map/while/body/eval_jaxpr/ppermute | solution.py:9
  92.6 5.5 %collective-permute-done = bf16[1024,256]{1,0:T(8,128)(2,1)S(1)} collective-permute-done((bf16[1024,256]{1,0:T(8,128)(2,1)S(1)}, bf16[1024,256]{1,0:T(8,128)(2,1)S(1)}, u32[]{:S(2)}, u32[]{:S(2)}) %collective-permute-start) | collective-permute-done | bytes 524320 | tf_op jit(solution)/shard_map/while/body/eval_jaxpr/ppermute | solution.py:9
  113.7 5.5 %collective-permute-done = bf16[1024,256]{1,0:T(8,128)(2,1)S(1)} collective-permute-done((bf16[1024,256]{1,0:T(8,128)(2,1)S(1)}, bf16[1024,256]{1,0:T(8,128)(2,1)S(1)}, u32[]{:S(2)}, u32[]{:S(2)}) %collective-permute-start) | collective-permute-done | bytes 524320 | tf_op jit(solution)/shard_map/while/body/eval_jaxpr/ppermute | solution.py:9
  134.9 5.5 %collective-permute-done = bf16[1024,256]{1,0:T(8,128)(2,1)S(1)} collective-permute-done((bf16[1024,256]{1,0:T(8,128)(2,1)S(1)}, bf16[1024,256]{1,0:T(8,128)(2,1)S(1)}, u32[]{:S(2)}, u32[]{:S(2)}) %collective-permute-start) | collective-permute-done | bytes 524320 | tf_op jit(solution)/shard_map/while/body/eval_jaxpr/ppermute | solution.py:9
  156.0 5.5 %collective-permute-done = bf16[1024,256]{1,0:T(8,128)(2,1)S(1)} collective-permute-done((bf16[1024,256]{1,0:T(8,128)(2,1)S(1)}, bf16[1024,256]{1,0:T(8,128)(2,1)S(1)}, u32[]{:S(2)}, u32[]{:S(2)}) %collective-permute-start) | collective-permute-done | bytes 524320 | tf_op jit(solution)/shard_map/while/body/eval_jaxpr/ppermute | solution.py:9
  177.1 5.5 %collective-permute-done = bf16[1024,256]{1,0:T(8,128)(2,1)S(1)} collective-permute-done((bf16[1024,256]{1,0:T(8,128)(2,1)S(1)}, bf16[1024,256]{1,0:T(8,128)(2,1)S(1)}, u32[]{:S(2)}, u32[]{:S(2)}) %collective-permute-start) | collective-permute-done | bytes 524320 | tf_op jit(solution)/shard_map/while/body/eval_jaxpr/ppermute | solution.py:9
  194.0 23.9 %all-reduce.8 = bf16[1024,256]{1,0:T(8,128)(2,1)S(1)} all-reduce(f32[1024,256]{1,0:T(8,128)S(1)} %bitcast.97), channel_id=1, replica_groups=mesh['blk'=16,'rep'=2] {'rep'}, use_global_device_ids=true, to_apply=%region_2.5 | all-reduce | flops 262144 | bytes 1572864 | tf_op jit(solution)/shard_map/psum | solution.py:89
  231.6 148.3 %while.33 = (s32[]{:T(128)}, f32[8,128,256]{2,0,1:T(8,128)}, s32[8,64]{1,0:T(8,128)}, s32[8]{0:T(128)S(1)}, s32[8,64]{1,0:T(8,128)}, /*index=5*/bf16[128,128,128...) while((s32[]{:T(128)}, f32[8,128,256]{2,0,1:T(8,128)}, ...), condition=%wide.region_4.7_spmd, body=%wide.region_3.6_spmd.sunk | while | flops 573837120 | bytes 33566048 | solution.py:128
  244.4 4.6 fusion.119
  249.0 4.5 collective-permute-start.1
  266.2 4.6 fusion.119
  270.8 4.5 collective-permute-start.1
  288.0 4.6 fusion.119
  292.6 4.5 collective-permute-start.1
  309.9 4.6 fusion.119
  314.5 4.5 collective-permute-start.1
  331.7 4.6 fusion.119
  336.3 4.5 collective-permute-start.1
  349.4 4.1 fusion.117
  353.5 4.6 fusion.119
  358.1 4.5 collective-permute-start.1
  371.2 4.1 fusion.117
  375.4 4.6 fusion.119
  385.5 6.5 %collective-permute-done.3 = bf16[8,128,256]{2,0,1:T(8,128)(2,1)S(1)} collective-permute-done((bf16[8,128,256]{2,0,1:T(8,128)(2,1)S(1)}, bf16[8,128,256]{2,0,1:T(8,128)(2,1)S(1)}, u32[]{:S(2)}, u32[]{:S(2)}) %collective-permute-start.3) | collective-permute-done | bytes 524320 | tf_op jit(solution)/shard_map/ppermute | solution.py:9
  394.3 36.1 %psum.39 = bf16[256]{0:T(256)(128)(2,1)S(1)} all-reduce(bf16[256]{0:T(256)(128)(2,1)S(1)} %get-tuple-element.457), channel_id=1, replica_groups=mesh['blk'=16,'rep'=2] {'blk'}, use_global_device_ids=true, to_apply=%region_9.12 | all-reduce | flops 256 | bytes 1024 | tf_op jit(solution)/shard_map/psum | solution.py:119
  430.9 47.6 %all-reduce.7.cloned.1.call-done = (bf16[256,256]{0,1:T(8,128)(2,1)}, bf16[256,256]{1,0:T(8,128)(2,1)}) async-done(((bf16[256,256]{0,1:T(8,128)(2,1)}, bf16[256,256]{1,0:T(8,128)(2,1)}), (bf16[256,256]{0,1:T(8,128)(2,1)}, bf16[256,256]{1,0:T(8,128)(2,1)})) %all-reduce.7.cloned.1.call-update) | async-done | bytes 262160 | tf_op jit(solution)/shard_map/psum | solution.py:117
  481.9 28.7 %all-reduce.5.cloned.1.call-done = bf16[1024,256]{1,0:T(8,128)(2,1)} async-done(((bf16[1024,256]{1,0:T(8,128)(2,1)}), bf16[1024,256]{1,0:T(8,128)(2,1)}) %all-reduce.5.cloned.1.call-update) | async-done | bytes 524304 | tf_op jit(solution)/shard_map/psum | solution.py:135
  (235 shorter events, 238.5 us)
Async XLA Ops:
  7.2 210.7 %copy-start = (bf16[256,256]{1,0:T(8,128)(2,1)S(1)}, bf16[256,256]{1,0:T(8,128)(2,1)}, u32[]{:S(2)}) copy-start(bf16[256,256]{1,0:T(8,128)(2,1)} %param.20) | copy-start | bytes 393220
  7.2 471.4 %all-reduce.7.cloned.1.call-start = ((), (), s32[]{:S(2)}) async-start(), calls=%async_computation.1 | async-start | bytes 524288 | tf_op jit(solution)/shard_map/psum | solution.py:117
  7.2 27.6 %collective-permute-start.2 = (bf16[1024,256]{1,0:T(8,128)(2,1)}, bf16[1024,256]{1,0:T(8,128)(2,1)}, u32[]{:S(2)}, u32[]{:S(2)}) collective-permute-start(bf16[1024,256]{1,0:T(8,128)(2,1)} %param.18), channel_id=1, source_target_pairs={{0,16},{2,18},{4,20},{6,22},{8,24},{10,26},{12,28},{14,30},{16,0},... | collective-permute-start | bytes 1572872 | tf_op jit(solution)/shard_map/ppermute | solution.py:9
  16.2 8.3 %copy-start.4 = (bf16[1024,256]{1,0:T(8,128)(2,1)S(1)}, bf16[1024,256]{1,0:T(8,128)(2,1)}, u32[]{:S(2)}) copy-start(bf16[1024,256]{1,0:T(8,128)(2,1)} %param.18) | copy-start | bytes 1572868
  16.2 8.3 %copy-start.7 = (bf16[256,256]{1,0:T(8,128)(2,1)S(1)}, bf16[256,256]{1,0:T(8,128)(2,1)}, u32[]{:S(2)}) copy-start(bf16[256,256]{1,0:T(8,128)(2,1)} %param.19) | copy-start | bytes 393220
  41.2 3.4 copy-start.8
  44.6 173.3 %copy-start.9 = (f32[256]{0:T(256)S(1)}, f32[256]{0:T(256)}, u32[]{:S(2)}) copy-start(f32[256]{0:T(256)} %param.21) | copy-start | bytes 3076
  44.6 11.3 %collective-permute-start = (bf16[1024,256]{1,0:T(8,128)(2,1)S(1)}, bf16[1024,256]{1,0:T(8,128)(2,1)S(1)}, u32[]{:S(2)}, u32[]{:S(2)}) collective-permute-start(bf16[1024,256]{1,0:T(8,128)(2,1)S(1)} %get-tuple-element.605), channel_id=1, source_target_pairs={{0,2},{2,4},{4,6},{6,8},{8,10},{10,12},{12,14},{14,16},{16,18},{18... | collective-permute-start | bytes 1572872 | tf_op jit(solution)/shard_map/while/body/eval_jaxpr/ppermute | solution.py:9
  58.7 3.6 copy-start.1
  65.7 11.3 %collective-permute-start = (bf16[1024,256]{1,0:T(8,128)(2,1)S(1)}, bf16[1024,256]{1,0:T(8,128)(2,1)S(1)}, u32[]{:S(2)}, u32[]{:S(2)}) collective-permute-start(bf16[1024,256]{1,0:T(8,128)(2,1)S(1)} %get-tuple-element.605), channel_id=1, source_target_pairs={{0,2},{2,4},{4,6},{6,8},{8,10},{10,12},{12,14},{14,16},{16,18},{18... | collective-permute-start | bytes 1572872 | tf_op jit(solution)/shard_map/while/body/eval_jaxpr/ppermute | solution.py:9
  79.8 3.6 copy-start.1
  86.8 11.3 %collective-permute-start = (bf16[1024,256]{1,0:T(8,128)(2,1)S(1)}, bf16[1024,256]{1,0:T(8,128)(2,1)S(1)}, u32[]{:S(2)}, u32[]{:S(2)}) collective-permute-start(bf16[1024,256]{1,0:T(8,128)(2,1)S(1)} %get-tuple-element.605), channel_id=1, source_target_pairs={{0,2},{2,4},{4,6},{6,8},{8,10},{10,12},{12,14},{14,16},{16,18},{18... | collective-permute-start | bytes 1572872 | tf_op jit(solution)/shard_map/while/body/eval_jaxpr/ppermute | solution.py:9
  100.9 3.6 copy-start.1
  107.9 11.3 %collective-permute-start = (bf16[1024,256]{1,0:T(8,128)(2,1)S(1)}, bf16[1024,256]{1,0:T(8,128)(2,1)S(1)}, u32[]{:S(2)}, u32[]{:S(2)}) collective-permute-start(bf16[1024,256]{1,0:T(8,128)(2,1)S(1)} %get-tuple-element.605), channel_id=1, source_target_pairs={{0,2},{2,4},{4,6},{6,8},{8,10},{10,12},{12,14},{14,16},{16,18},{18... | collective-permute-start | bytes 1572872 | tf_op jit(solution)/shard_map/while/body/eval_jaxpr/ppermute | solution.py:9
  122.0 3.6 copy-start.1
  129.0 11.3 %collective-permute-start = (bf16[1024,256]{1,0:T(8,128)(2,1)S(1)}, bf16[1024,256]{1,0:T(8,128)(2,1)S(1)}, u32[]{:S(2)}, u32[]{:S(2)}) collective-permute-start(bf16[1024,256]{1,0:T(8,128)(2,1)S(1)} %get-tuple-element.605), channel_id=1, source_target_pairs={{0,2},{2,4},{4,6},{6,8},{8,10},{10,12},{12,14},{14,16},{16,18},{18... | collective-permute-start | bytes 1572872 | tf_op jit(solution)/shard_map/while/body/eval_jaxpr/ppermute | solution.py:9
  143.1 3.6 copy-start.1
  150.2 11.3 %collective-permute-start = (bf16[1024,256]{1,0:T(8,128)(2,1)S(1)}, bf16[1024,256]{1,0:T(8,128)(2,1)S(1)}, u32[]{:S(2)}, u32[]{:S(2)}) collective-permute-start(bf16[1024,256]{1,0:T(8,128)(2,1)S(1)} %get-tuple-element.605), channel_id=1, source_target_pairs={{0,2},{2,4},{4,6},{6,8},{8,10},{10,12},{12,14},{14,16},{16,18},{18... | collective-permute-start | bytes 1572872 | tf_op jit(solution)/shard_map/while/body/eval_jaxpr/ppermute | solution.py:9
  164.2 3.6 copy-start.1
  171.3 11.3 %collective-permute-start = (bf16[1024,256]{1,0:T(8,128)(2,1)S(1)}, bf16[1024,256]{1,0:T(8,128)(2,1)S(1)}, u32[]{:S(2)}, u32[]{:S(2)}) collective-permute-start(bf16[1024,256]{1,0:T(8,128)(2,1)S(1)} %get-tuple-element.605), channel_id=1, source_target_pairs={{0,2},{2,4},{4,6},{6,8},{8,10},{10,12},{12,14},{14,16},{16,18},{18... | collective-permute-start | bytes 1572872 | tf_op jit(solution)/shard_map/while/body/eval_jaxpr/ppermute | solution.py:9
  185.4 3.6 copy-start.1
  194.0 26.7 %copy-start.5 = (bf16[1024,256]{1,0:T(8,128)(2,1)S(1)}, bf16[1024,256]{1,0:T(8,128)(2,1)}, u32[]{:S(2)}) copy-start(bf16[1024,256]{1,0:T(8,128)(2,1)} %param.27) | copy-start | bytes 1572868
  217.9 3.5 copy-start.6
  231.6 12.7 %collective-permute-start.1 = (f32[8,128,256]{2,0,1:T(8,128)}, f32[8,128,256]{2,0,1:T(8,128)}, u32[]{:S(2)}, u32[]{:S(2)}) collective-permute-start(f32[8,128,256]{2,0,1:T(8,128)} %get-tuple-element.639), channel_id=1, source_target_pairs={{0,30},{2,0},{4,2},{6,4},{8,6},{10,8},{12,10},{14,12},{16,14},{18,... | collective-permute-start | bytes 3145736 | tf_op jit(solution)/shard_map/while/body/eval_jaxpr/ppermute | solution.py:9
  249.0 17.2 %collective-permute-start.1 = (f32[8,128,256]{2,0,1:T(8,128)}, f32[8,128,256]{2,0,1:T(8,128)}, u32[]{:S(2)}, u32[]{:S(2)}) collective-permute-start(f32[8,128,256]{2,0,1:T(8,128)} %get-tuple-element.639), channel_id=1, source_target_pairs={{0,30},{2,0},{4,2},{6,4},{8,6},{10,8},{12,10},{14,12},{16,14},{18,... | collective-permute-start | bytes 3145736 | tf_op jit(solution)/shard_map/while/body/eval_jaxpr/ppermute | solution.py:9
  270.8 17.2 %collective-permute-start.1 = (f32[8,128,256]{2,0,1:T(8,128)}, f32[8,128,256]{2,0,1:T(8,128)}, u32[]{:S(2)}, u32[]{:S(2)}) collective-permute-start(f32[8,128,256]{2,0,1:T(8,128)} %get-tuple-element.639), channel_id=1, source_target_pairs={{0,30},{2,0},{4,2},{6,4},{8,6},{10,8},{12,10},{14,12},{16,14},{18,... | collective-permute-start | bytes 3145736 | tf_op jit(solution)/shard_map/while/body/eval_jaxpr/ppermute | solution.py:9
  292.6 17.2 %collective-permute-start.1 = (f32[8,128,256]{2,0,1:T(8,128)}, f32[8,128,256]{2,0,1:T(8,128)}, u32[]{:S(2)}, u32[]{:S(2)}) collective-permute-start(f32[8,128,256]{2,0,1:T(8,128)} %get-tuple-element.639), channel_id=1, source_target_pairs={{0,30},{2,0},{4,2},{6,4},{8,6},{10,8},{12,10},{14,12},{16,14},{18,... | collective-permute-start | bytes 3145736 | tf_op jit(solution)/shard_map/while/body/eval_jaxpr/ppermute | solution.py:9
  314.5 17.2 %collective-permute-start.1 = (f32[8,128,256]{2,0,1:T(8,128)}, f32[8,128,256]{2,0,1:T(8,128)}, u32[]{:S(2)}, u32[]{:S(2)}) collective-permute-start(f32[8,128,256]{2,0,1:T(8,128)} %get-tuple-element.639), channel_id=1, source_target_pairs={{0,30},{2,0},{4,2},{6,4},{8,6},{10,8},{12,10},{14,12},{16,14},{18,... | collective-permute-start | bytes 3145736 | tf_op jit(solution)/shard_map/while/body/eval_jaxpr/ppermute | solution.py:9
  336.3 17.2 %collective-permute-start.1 = (f32[8,128,256]{2,0,1:T(8,128)}, f32[8,128,256]{2,0,1:T(8,128)}, u32[]{:S(2)}, u32[]{:S(2)}) collective-permute-start(f32[8,128,256]{2,0,1:T(8,128)} %get-tuple-element.639), channel_id=1, source_target_pairs={{0,30},{2,0},{4,2},{6,4},{8,6},{10,8},{12,10},{14,12},{16,14},{18,... | collective-permute-start | bytes 3145736 | tf_op jit(solution)/shard_map/while/body/eval_jaxpr/ppermute | solution.py:9
  358.1 17.2 %collective-permute-start.1 = (f32[8,128,256]{2,0,1:T(8,128)}, f32[8,128,256]{2,0,1:T(8,128)}, u32[]{:S(2)}, u32[]{:S(2)}) collective-permute-start(f32[8,128,256]{2,0,1:T(8,128)} %get-tuple-element.639), channel_id=1, source_target_pairs={{0,30},{2,0},{4,2},{6,4},{8,6},{10,8},{12,10},{14,12},{16,14},{18,... | collective-permute-start | bytes 3145736 | tf_op jit(solution)/shard_map/while/body/eval_jaxpr/ppermute | solution.py:9
  381.2 10.8 %collective-permute-start.3 = (bf16[8,128,256]{2,0,1:T(8,128)(2,1)S(1)}, bf16[8,128,256]{2,0,1:T(8,128)(2,1)S(1)}, u32[]{:S(2)}, u32[]{:S(2)}) collective-permute-start(bf16[8,128,256]{2,0,1:T(8,128)(2,1)S(1)} %convert_element_type.66), channel_id=1, source_target_pairs={{0,16},{2,18},{4,20},{6,22},{8,24},{10,26},{12,28},{14,30},{16,0},... | collective-permute-start | bytes 1572872 | tf_op jit(solution)/shard_map/ppermute | solution.py:9
  385.4 125.2 %all-reduce.5.cloned.1.call-start = ((), (), s32[]{:S(2)}) async-start(), calls=%async_computation | async-start | bytes 1048576 | tf_op jit(solution)/shard_map/psum | solution.py:135
  (8 other events, 10.1 us)
Sparse Core Ops, SparseCore 0:
  385.6 92.9 all-reduce.6
  481.4 29.1 all-reduce.4
where the time goes:
time: 522 us; the launch traced here: 520 us
  waiting for transfers between devices  130 us (25%)
  local copies, waits for them, and re-layouts  128 us (25%)
  matrix products  127 us (24%)
  blocking collectives  60 us (11%)
  starting transfers between devices  31.5 us (6%)
  other arithmetic  27.4 us (5%)
  between operations  14.2 us (3%)
    dot_general x16, matrix products, gather_terms(): jnp.einsum('kr,kaf->raf', placing, products, preferred_element_type=jnp.f...  55.3 us
    ppermute x16, waiting for transfers between devices, from_behind(): lax.ppermute(array, axis, [(i, (i + by) % length) for i in range(length)])  54 us
    gather x16, local copies, waits for them, and re-layouts, gather_terms(): tile_values = jnp.take(tile_table, value_pick, axis=0)  51.5 us
    psum x1, waiting for transfers between devices, on_device(): lax.psum(grad_self.astype(jnp.bfloat16), 'blk').astype(jnp.float32)  47.6 us
    psum x1, blocking collectives, on_device(): lax.psum(grad_offset.astype(jnp.bfloat16), 'blk').astype(jnp.float32)  36.1 us
    dot_general x8, matrix products, gather_terms(): jnp.einsum('kab,kaf->kbf', tile_values, picked, preferred_element_type=jn...  32.8 us
    ppermute x16, starting transfers between devices, from_behind(): lax.ppermute(array, axis, [(i, (i + by) % length) for i in range(length)])  31.5 us
    dot_general x8, matrix products, gather_terms(): jnp.einsum('kab,kbf->kaf', tile_values, picked, preferred_element_type=jn...  28.7 us
  transfers between devices with their start and end apart: 18, of which 11 were waited for; matrix products, arithmetic and copies ran while one was open for 30% of the time, Pallas kernels for 0%

commit v1 on v0

v1 whole, which is shorter than its diff:
```python
import functools

import jax
import jax.numpy as jnp
from jax import lax
from jax.experimental import pallas as pl
from jax.experimental.pallas import tpu as pltpu
from jax.sharding import PartitionSpec as P

ROWS_ROWS = (((0,), (0,)), ((), ()))
COLS_COLS = (((1,), (1,)), ((), ()))


def build_kernel(rows, columns, values, counts, table, dense):
    step = pl.program_id(0)
    tile = table.shape[1]
    dense[...] = jnp.zeros_like(dense)

    def add_tile(slot, carry):
        row = pl.multiple_of(rows[step, slot] * tile, tile)
        column = pl.multiple_of(columns[step, slot] * tile, tile)
        place = (0, pl.ds(row, tile), pl.ds(column, tile))
        dense[place] = dense[place] + table[values[step, slot]]
        return carry

    lax.fori_loop(0, counts[step], add_tile, 0)


def build_dense(rows, columns, values, counts, table, row_total):
    step_count = rows.shape[0]
    return pl.pallas_call(
        build_kernel,
        grid_spec=pltpu.PrefetchScalarGridSpec(
            num_scalar_prefetch=4,
            grid=(step_count,),
            in_specs=[pl.BlockSpec(table.shape, lambda s, *_: (0, 0, 0))],
            out_specs=pl.BlockSpec((1, row_total, row_total), lambda s, *_: (s, 0, 0)),
        ),
        out_shape=jax.ShapeDtypeStruct((step_count, row_total, row_total), jnp.bfloat16),
        cost_estimate=pl.CostEstimate(
            flops=0, bytes_accessed=20 * 2**20, transcendentals=0
        ),
        name="build",
    )(rows, columns, values, counts, table)


def forward_kernel(sources, dense, panel, out, total):
    step = pl.program_id(0)
    term = jnp.dot(dense[0], panel[0], preferred_element_type=jnp.float32)

    @pl.when(step == 0)
    def _():
        total[...] = term

    @pl.when(step > 0)
    def _():
        total[...] += term

    @pl.when(step == pl.num_programs(0) - 1)
    def _():
        out[...] = total[...].astype(out.dtype)


def forward(sources, dense, panels):
    step_count, row_total, _ = dense.shape
    width = panels.shape[2]
    return pl.pallas_call(
        forward_kernel,
        grid_spec=pltpu.PrefetchScalarGridSpec(
            num_scalar_prefetch=1,
            grid=(step_count,),
            in_specs=[
                pl.BlockSpec((1, row_total, row_total), lambda s, src: (s, 0, 0)),
                pl.BlockSpec((1, row_total, width), lambda s, src: (src[s], 0, 0)),
            ],
            out_specs=pl.BlockSpec((row_total, width), lambda s, src: (0, 0)),
            scratch_shapes=[pltpu.VMEM((row_total, width), jnp.float32)],
        ),
        out_shape=jax.ShapeDtypeStruct((row_total, width), jnp.bfloat16),
        name="forward",
    )(sources, dense, panels)


def layer_kernel(
    features, mine, other, weight_self, weight_neighbor, bias, cotangent,
    activations, sent_t, self_t, grads,
):
    f32 = jnp.float32
    width = features.shape[1]
    aggregate = (mine[...].astype(f32) + other[...].astype(f32)).astype(jnp.bfloat16)
    pre = (
        jnp.dot(features[...], weight_self[...], preferred_element_type=f32)
        + jnp.dot(aggregate, weight_neighbor[...], preferred_element_type=f32)
        + bias[...]
    )
    sigmoid = jax.nn.sigmoid(pre)
    activations[...] = (pre * sigmoid).astype(activations.dtype)
    derivative = sigmoid * (1.0 + pre * (1.0 - sigmoid))
    grad_pre = (cotangent[...].astype(f32) * derivative).astype(jnp.bfloat16)
    sent_t[...] = lax.dot_general(
        weight_neighbor[...], grad_pre, COLS_COLS, preferred_element_type=f32
    ).astype(sent_t.dtype)
    self_t[...] = lax.dot_general(
        weight_self[...], grad_pre, COLS_COLS, preferred_element_type=f32
    )
    grads[0:width, :] = lax.dot_general(
        features[...], grad_pre, ROWS_ROWS, preferred_element_type=f32
    ).astype(grads.dtype)
    grads[width : 2 * width, :] = lax.dot_general(
        aggregate, grad_pre, ROWS_ROWS, preferred_element_type=f32
    ).astype(grads.dtype)
    summed = jnp.sum(grad_pre.astype(f32), axis=0, keepdims=True)
    tail = grads.shape[0] - 2 * width
    grads[2 * width :, :] = jnp.broadcast_to(summed, (tail, width)).astype(grads.dtype)


def layer(features, mine, other, weight_self, weight_neighbor, bias, cotangent):
    row_total, width = features.shape
    shape = jax.ShapeDtypeStruct
    return pl.pallas_call(
        layer_kernel,
        out_shape=(
            shape((row_total, width), jnp.bfloat16),
            shape((width, row_total), jnp.bfloat16),
            shape((width, row_total), jnp.float32),
            shape((2 * width + 32, width), jnp.bfloat16),
        ),
        name="layer",
    )(features, mine, other, weight_self, weight_neighbor, bias, cotangent)


def backward_kernel(step_count, targets, dense, sent_t, out):
    step = pl.program_id(0)

    @pl.when(step < step_count)
    def _():
        out[0] = jnp.dot(
            sent_t[...], dense[0], preferred_element_type=jnp.float32
        ).astype(out.dtype)

    @pl.when(step >= step_count)
    def _():
        out[...] = jnp.zeros_like(out)


def backward(targets, dense, sent_t):
    step_count, row_total, _ = dense.shape
    width = sent_t.shape[0]
    cycle = targets.shape[0]
    return pl.pallas_call(
        functools.partial(backward_kernel, step_count),
        grid_spec=pltpu.PrefetchScalarGridSpec(
            num_scalar_prefetch=1,
            grid=(cycle,),
            in_specs=[
                pl.BlockSpec(
                    (1, row_total, row_total),
                    lambda s, dst: (jnp.minimum(s, step_count - 1), 0, 0),
                ),
                pl.BlockSpec((width, row_total), lambda s, dst: (0, 0)),
            ],
            out_specs=pl.BlockSpec((1, width, row_total), lambda s, dst: (dst[s], 0, 0)),
        ),
        out_shape=jax.ShapeDtypeStruct((cycle, width, row_total), jnp.bfloat16),
        name="backward",
    )(targets, dense, sent_t)


def on_device(
    features,
    weight_self,
    weight_neighbor,
    bias_vector,
    tile_row,
    tile_column,
    tile_value,
    tile_count,
    tile_table,
    cotangent,
):
    f32, bf16 = jnp.float32, jnp.bfloat16
    cycle_length = lax.axis_size("blk")
    replicas = lax.axis_size("rep")
    step_count = cycle_length // replicas
    group = lax.axis_index("blk")
    replica = lax.axis_index("rep")
    row_total, width = features.shape

    panels = lax.all_gather(features, "blk")
    dense = build_dense(
        tile_row[0], tile_column[0], tile_value[0], tile_count[0], tile_table, row_total
    )
    reached = jnp.mod(
        group - replica * step_count - jnp.arange(cycle_length, dtype=jnp.int32),
        cycle_length,
    ).astype(jnp.int32)
    mine = forward(reached[:step_count], dense, panels)
    bit = 1
    while True:
        other = lax.ppermute(mine, "rep", [(i, i ^ bit) for i in range(replicas)])
        bit *= 2
        if bit >= replicas:
            break
        mine = (mine.astype(f32) + other.astype(f32)).astype(bf16)
    activations, sent_t, self_t, grads = layer(
        features, mine, other, weight_self, weight_neighbor,
        bias_vector.reshape(1, width), cotangent,
    )
    partial = backward(reached, dense, sent_t)
    pushed = lax.psum_scatter(partial, "blk", scatter_dimension=0)
    grads = lax.psum(grads, "blk").astype(f32)
    bit = 1
    while bit < replicas:
        other = lax.ppermute(pushed, "rep", [(i, i ^ bit) for i in range(replicas)])
        pushed = (pushed.astype(f32) + other.astype(f32)).astype(
            bf16 if 2 * bit < replicas else f32
        )
        bit *= 2
    grad_features = (self_t + pushed).astype(bf16).T
    return (
        activations,
        grad_features,
        grads[:width],
        grads[width : 2 * width],
        grads[2 * width],
    )


def solution(mesh):
    placed = (
        P("blk", None),
        P(),
        P(),
        P(),
        P("blk", "rep", None),
        P("blk", "rep", None),
        P("blk", "rep", None),
        P("blk", "rep"),
        P(("blk", "rep"), None, None),
        P("blk", None),
    )
    return jax.shard_map(
        on_device,
        mesh=mesh,
        in_specs=placed,
        out_specs=(P("blk", None), P("blk", None), P(), P(), P()),
        check_vma=False,
    )
```

time: 522 us -> 343 us (0.66)
  waiting for transfers between devices: 130 us -> 273 us
  matrix products: 127 us -> 0 us
  local copies, waits for them, and re-layouts: 128 us -> 4.84 us
  blocking collectives: 60 us -> 0 us
  Pallas kernels: 0 us -> 46 us
  starting transfers between devices: 31.5 us -> 3.07 us
  other arithmetic: 27.4 us -> 1.79 us
    dot_general x38 -> x0, matrix products: 127 us -> none  [the longest x16 55.3 us: gather_terms(): jnp.einsum('kr,kaf->raf', placing, products, preferred_element_type=jnp.f...]
    reduce_scatter x0 -> x1, waiting for transfers between devices: none -> 102 us  [on_device(): pushed = lax.psum_scatter(partial, 'blk', scatter_dimension=0)]
    gather x32 -> x0, local copies, waits for them, and re-layouts: 96 us -> none  [the longest x16 51.5 us: gather_terms(): tile_values = jnp.take(tile_table, value_pick, axis=0)]
    all_gather x0 -> x1, waiting for transfers between devices: none -> 65.7 us  [on_device(): panels = lax.all_gather(features, 'blk')]
    psum x2 -> x0, blocking collectives: 60 us -> none  [the longest x1 36.1 us: on_device(): lax.psum(grad_offset.astype(jnp.bfloat16), 'blk').astype(jnp.float32)]
    pallas_call x0 -> x4, Pallas kernels: none -> 46 us  [the longest x1 16 us: backward(): pl.pallas_call(functools.partial(backward_kernel, step_count), grid_spec=...]
    ppermute x16 -> x2, waiting for transfers between devices: 54 us -> 12.8 us  [the longest x1 12.8 us: on_device(): other = lax.ppermute(mine, 'rep', [(i, i ^ bit) for i in range(replicas)])]
    ppermute x16 -> x2, starting transfers between devices: 31.5 us -> 2.95 us  [the longest x1 1.49 us: on_device(): other = lax.ppermute(pushed, 'rep', [(i, i ^ bit) for i in range(replicas)])]
  transfers between devices with their start and end apart: 18 -> 5, of which waited for: 11 -> 4; matrix products, arithmetic and copies ran while one was open for 30% -> 1% of each run, Pallas kernels for 0% -> 4%
where the time goes in v1:
time: 343 us
  waiting for transfers between devices  273 us (80%)
  Pallas kernels  46 us (13%)
  between operations  13.8 us (4%)
  local copies, waits for them, and re-layouts  4.84 us (1%)
    reduce_scatter x1, waiting for transfers between devices, on_device(): pushed = lax.psum_scatter(partial, 'blk', scatter_dimension=0)  102 us
    psum x1, waiting for transfers between devices, on_device(): grads = lax.psum(grads, 'blk').astype(f32)  92 us
    all_gather x1, waiting for transfers between devices, on_device(): panels = lax.all_gather(features, 'blk')  65.7 us
    pallas_call x1, Pallas kernels, backward(): pl.pallas_call(functools.partial(backward_kernel, step_count), grid_spec=...  16 us
    pallas_call x1, Pallas kernels, build_dense(): pl.pallas_call(build_kernel, grid_spec=pltpu.PrefetchScalarGridSpec(num_s...  13.1 us
    pallas_call x1, Pallas kernels, forward(): pl.pallas_call(forward_kernel, grid_spec=pltpu.PrefetchScalarGridSpec(num...  12.8 us
    ppermute x1, waiting for transfers between devices, on_device(): other = lax.ppermute(mine, 'rep', [(i, i ^ bit) for i in range(replicas)])  12.8 us
  transfers between devices with their start and end apart: 5, of which 4 were waited for; matrix products, arithmetic and copies ran while one was open for 1% of the time, Pallas kernels for 4%

profile of v1, /device:TPU:0, one launch (start us, length us, event | category | flops | bytes accessed | tf_op | source)
XLA Modules:
  0.0 342.8 jit_solution(11090739747097458531)
XLA Ops:
  7.2 0.0 all-gather.3.cloned.1.call-start
  7.2 0.7 all-gather.3.cloned.1.call-update
  7.9 0.0 reduce-scatter.2.cloned.1.call-start
  8.0 13.1 %build.1.dense = bf16[8,1024,1024]{2,1,0:T(8,128)(2,1)} custom-call(s32[8,64]{1,0:T(8,128)} %bitcast.14, s32[8,64]{1,0:T(8,128)} %bitcast.15, s32[8,64]{1,0:T(8,128)} %bitcast.16, s32[8]{0:T(128)} %bitcast.20, bf16[128,128,128]{2,1,0:T(8,128)(2,1)} %table.1), custom_call_target="tpu_custom_call" | custom-call | bytes 20971520 | tf_op jit(solution)/shard_map/build/pallas_call | solution.py:31
  21.0 0.5 and_select_fusion.targets
  21.5 65.7 %all-gather.3.cloned.1.call-done = bf16[16384,256]{1,0:T(8,128)(2,1)} async-done(((bf16[1024,256]{1,0:T(8,128)(2,1)}), bf16[16384,256]{1,0:T(8,128)(2,1)}) %all-gather.3.cloned.1.call-update) | async-done | bytes 8388624 | tf_op jit(solution)/shard_map/all_gather | solution.py:189
  87.2 12.8 %forward.1.mine = bf16[1024,256]{1,0:T(8,128)(2,1)} custom-call(s32[8]{0:T(128)} %bitcast.17, bf16[8,1024,1024]{2,1,0:T(8,128)(2,1)} %build.1.dense, bf16[16,1024,256]{2,1,0:T(8,128)(2,1)} %bitcast.12), custom_call_target="tpu_custom_call" | custom-call | tf_op jit(solution)/shard_map/forward/pallas_call | solution.py:67
  100.0 1.5 collective-permute-start
  101.5 12.8 %collective-permute-done.other = bf16[1024,256]{1,0:T(8,128)(2,1)S(1)} collective-permute-done((bf16[1024,256]{1,0:T(8,128)(2,1)}, bf16[1024,256]{1,0:T(8,128)(2,1)S(1)}, u32[]{:S(2)}, u32[]{:S(2)}) %collective-permute-start) | collective-permute-done | bytes 524320 | tf_op jit(solution)/shard_map/ppermute | solution.py:200
  114.3 0.0 copy-start.1
  114.3 0.8 copy-done.1
  115.1 4.1 %layer.1 = (bf16[1024,256]{1,0:T(8,128)(2,1)}, bf16[256,1024]{1,0:T(8,128)(2,1)}, f32[256,1024]{1,0:T(8,128)}, bf16[544,256]{1,0:T(8,128)(2,1)}) custom-call(bf16[1024,256]{1,0:T(8,128)(2,1)} %features.1, bf16[1024,256]{1,0:T(8,128)(2,1)} %forward.1.mine, bf16[1024,256]{1,0:T(8,128)(2,1)} %copy-done.1, bf16[256,256]{1,0:T(8,128)(2,1)} %weight_self.1, ...), custom_call_target="tpu_custom_call" | custom-call | tf_op jit(solution)/shard_map/layer/pallas_call | solution.py:120
  119.2 16.0 %backward.1 = bf16[16,256,1024]{2,1,0:T(8,128)(2,1)} custom-call(s32[16]{0:T(128)} %and_select_fusion.targets, bf16[8,1024,1024]{2,1,0:T(8,128)(2,1)} %build.1.dense, bf16[256,1024]{1,0:T(8,128)(2,1)} %get-tuple-element.11.sent_t), custom_call_target="tpu_custom_call" | custom-call | tf_op jit(solution)/shard_map/backward/pallas_call | solution.py:150
  135.2 0.0 copy-start
  135.2 0.0 reduce-scatter.2.cloned.1.call-update
  135.2 0.0 all-reduce.2.cloned.1.call-start
  135.3 102.2 %reduce-scatter.2.cloned.1.call-done = bf16[1,256,1024]{2,1,0:T(8,128)(2,1)} async-done(((bf16[16,256,1024]{2,1,0:T(8,128)(2,1)}), bf16[1,256,1024]{2,1,0:T(8,128)(2,1)}) %reduce-scatter.2.cloned.1.call-update) | async-done | bytes 524304 | tf_op jit(solution)/shard_map/reduce_scatter | solution.py:210
  237.4 1.5 collective-permute-start.1
  238.9 0.0 all-reduce.2.cloned.1.call-update
  239.0 92.0 %all-reduce.2.cloned.1.call-done = bf16[544,256]{1,0:T(8,128)(2,1)} async-done(((bf16[544,256]{1,0:T(8,128)(2,1)}), bf16[544,256]{1,0:T(8,128)(2,1)}) %all-reduce.2.cloned.1.call-update) | async-done | bytes 278544 | tf_op jit(solution)/shard_map/psum | solution.py:211
  330.9 1.2 slice.18
  332.2 1.8 fusion.2
  333.9 0.0 collective-permute-done.1
  334.0 0.0 copy-done
  334.0 1.3 fusion
  335.2 1.0 copy.15
Async XLA Ops:
  7.2 80.0 %all-gather.3.cloned.1.call-start = ((), (), s32[]{:S(2)}) async-start(), calls=%async_computation.3 | async-start | bytes 8912896 | tf_op jit(solution)/shard_map/all_gather | solution.py:189
  7.9 229.5 %reduce-scatter.2.cloned.1.call-start = ((), (), s32[]{:S(2)}) async-start(), calls=%async_computation.1 | async-start | bytes 8912896 | tf_op jit(solution)/shard_map/reduce_scatter | solution.py:210
  100.0 14.3 %collective-permute-start = (bf16[1024,256]{1,0:T(8,128)(2,1)}, bf16[1024,256]{1,0:T(8,128)(2,1)S(1)}, u32[]{:S(2)}, u32[]{:S(2)}) collective-permute-start(bf16[1024,256]{1,0:T(8,128)(2,1)} %forward.1.mine), channel_id=1, source_target_pairs={{0,1},{1,0},{2,3},{3,2},{4,5},{5,4},{6,7},{7,6},{8,9},{9,8},{10,11... | collective-permute-start | bytes 1572872 | tf_op jit(solution)/shard_map/ppermute | solution.py:200
  114.3 0.8 copy-start.1
  135.2 198.8 %copy-start = (f32[256,1024]{1,0:T(8,128)S(1)}, f32[256,1024]{1,0:T(8,128)}, u32[]{:S(2)}) copy-start(f32[256,1024]{1,0:T(8,128)} %get-tuple-element.10) | copy-start | bytes 3145732
  135.2 195.7 %all-reduce.2.cloned.1.call-start = ((), (), s32[]{:S(2)}) async-start(), calls=%async_computation.2 | async-start | bytes 557056 | tf_op jit(solution)/shard_map/psum | solution.py:211
  237.4 96.5 %collective-permute-start.1 = (bf16[256,1024]{1,0:T(8,128)(2,1)}, bf16[256,1024]{1,0:T(8,128)(2,1)S(1)}, u32[]{:S(2)}, u32[]{:S(2)}) collective-permute-start(bf16[256,1024]{1,0:T(8,128)(2,1)} %bitcast.13), channel_id=1, source_target_pairs={{0,1},{1,0},{2,3},{3,2},{4,5},{5,4},{6,7},{7,6},{8,9},{9,8},{10,11... | collective-permute-start | bytes 1572872 | tf_op jit(solution)/shard_map/ppermute | solution.py:214
Sparse Core Ops, SparseCore 0:
  10.1 77.0 all-gather.2
  135.3 102.0 reduce-scatter.1
  240.8 90.0 all-reduce.1

commit v2 on v1

v2 whole, which is shorter than its diff:
```python
import functools

import jax
import jax.numpy as jnp
from jax import lax
from jax.experimental import pallas as pl
from jax.experimental.pallas import tpu as pltpu
from jax.sharding import PartitionSpec as P

ROWS_ROWS = (((0,), (0,)), ((), ()))
COLS_COLS = (((1,), (1,)), ((), ()))


def build_kernel(rows, columns, values, counts, table, dense):
    step = pl.program_id(0)
    tile = table.shape[1]
    dense[...] = jnp.zeros_like(dense)

    def add_tile(slot, carry):
        row = pl.multiple_of(rows[step, slot] * tile, tile)
        column = pl.multiple_of(columns[step, slot] * tile, tile)
        place = (0, pl.ds(row, tile), pl.ds(column, tile))
        dense[place] = dense[place] + table[values[step, slot]]
        return carry

    lax.fori_loop(0, counts[step], add_tile, 0)


def build_dense(rows, columns, values, counts, table, row_total):
    step_count = rows.shape[0]
    return pl.pallas_call(
        build_kernel,
        grid_spec=pltpu.PrefetchScalarGridSpec(
            num_scalar_prefetch=4,
            grid=(step_count,),
            in_specs=[pl.BlockSpec(table.shape, lambda s, *_: (0, 0, 0))],
            out_specs=pl.BlockSpec((1, row_total, row_total), lambda s, *_: (s, 0, 0)),
        ),
        out_shape=jax.ShapeDtypeStruct((step_count, row_total, row_total), jnp.bfloat16),
        cost_estimate=pl.CostEstimate(
            flops=0, bytes_accessed=20 * 2**20, transcendentals=0
        ),
        name="build",
    )(rows, columns, values, counts, table)


def ring_place(cycle, replicas):
    group = lax.axis_index("blk")
    replica = lax.axis_index("rep")
    reverse = (2 * replica) // replicas if replicas > 1 else 0 * replica
    ahead = lax.rem(group + 1 - 2 * reverse + cycle, cycle)
    behind = lax.rem(group - 1 + 2 * reverse + cycle, cycle)
    return group, replica, reverse, ahead, behind


def greet(devices):
    barrier = pltpu.get_barrier_semaphore()
    for device in devices:
        pl.semaphore_signal(
            barrier, inc=1, device_id={"blk": device},
            device_id_type=pl.DeviceIdType.MESH,
        )
    pl.semaphore_wait(barrier, len(devices))


def forward_kernel(
    cycle, replicas, pieces, features, dense, out,
    slots, blocks, total, block_sem, first_sem, send_sem, recv_sem,
):
    steps, rows = blocks.shape[0], blocks.shape[1]
    _, _, reverse, ahead, behind = ring_place(cycle, replicas)
    size = rows // pieces
    first = pltpu.make_async_copy(features, slots.at[0], first_sem)
    first.start()

    def load(step):
        return pltpu.make_async_copy(
            dense.at[step], blocks.at[step], block_sem.at[step]
        )

    def in_order(hop):
        return hop * (1 - reverse) + (steps - hop) * reverse

    @pl.loop(0, steps)
    def _(hop):
        load(in_order(hop + reverse)).start()

    greet((ahead, behind))
    first.wait()

    def hop_copy(hop, piece):
        span = pl.ds(piece * size, size)
        return pltpu.make_async_remote_copy(
            src_ref=slots.at[hop, span],
            dst_ref=slots.at[hop + 1, span],
            send_sem=send_sem.at[hop, piece],
            recv_sem=recv_sem.at[hop, piece],
            device_id={"blk": ahead},
            device_id_type=pl.DeviceIdType.MESH,
        )

    total[...] = jnp.zeros_like(total)
    hops = steps - 1 + reverse

    @pl.loop(0, hops + 1)
    def _(hop):
        for piece in range(pieces):
            @pl.when(hop > 0)
            def _():
                hop_copy(hop - 1, piece).wait_recv()

            @pl.when(hop < hops)
            def _():
                hop_copy(hop, piece).start()

        step = in_order(hop)

        @pl.when(step < steps)
        def _():
            load(step).wait()
            total[...] += jnp.dot(
                blocks[step], slots[hop], preferred_element_type=jnp.float32
            )

    out[...] = total[...].astype(out.dtype)

    @pl.loop(0, hops)
    def _(hop):
        for piece in range(pieces):
            hop_copy(hop, piece).wait_send()


def forward(cycle, replicas, features, dense):
    step_count, row_total, _ = dense.shape
    width = features.shape[1]
    pieces = 4
    return pl.pallas_call(
        functools.partial(forward_kernel, cycle, replicas, pieces),
        in_specs=[pl.BlockSpec(memory_space=pl.ANY)] * 2,
        out_specs=pl.BlockSpec(memory_space=pltpu.VMEM),
        out_shape=jax.ShapeDtypeStruct((row_total, width), jnp.bfloat16),
        scratch_shapes=[
            pltpu.VMEM((step_count + 1, row_total, width), jnp.bfloat16),
            pltpu.VMEM(dense.shape, jnp.bfloat16),
            pltpu.VMEM((row_total, width), jnp.float32),
            pltpu.SemaphoreType.DMA((step_count,)),
            pltpu.SemaphoreType.DMA,
            pltpu.SemaphoreType.DMA((step_count, pieces)),
            pltpu.SemaphoreType.DMA((step_count, pieces)),
        ],
        compiler_params=pltpu.CompilerParams(collective_id=0, has_side_effects=True),
        name="forward",
    )(features, dense)


def layer_kernel(
    features, mine, other, weight_self, weight_neighbor, bias, cotangent,
    activations, sent_t, self_t, grads,
):
    f32 = jnp.float32
    width = features.shape[1]
    aggregate = (mine[...].astype(f32) + other[...].astype(f32)).astype(jnp.bfloat16)
    pre = (
        jnp.dot(features[...], weight_self[...], preferred_element_type=f32)
        + jnp.dot(aggregate, weight_neighbor[...], preferred_element_type=f32)
        + bias[...]
    )
    sigmoid = jax.nn.sigmoid(pre)
    activations[...] = (pre * sigmoid).astype(activations.dtype)
    derivative = sigmoid * (1.0 + pre * (1.0 - sigmoid))
    grad_pre = (cotangent[...].astype(f32) * derivative).astype(jnp.bfloat16)
    sent_t[...] = lax.dot_general(
        weight_neighbor[...], grad_pre, COLS_COLS, preferred_element_type=f32
    ).astype(sent_t.dtype)
    self_t[...] = lax.dot_general(
        weight_self[...], grad_pre, COLS_COLS, preferred_element_type=f32
    )
    grad_self = lax.dot_general(
        features[...], grad_pre, ROWS_ROWS, preferred_element_type=f32
    ).astype(grads.dtype)
    grad_neighbor = lax.dot_general(
        aggregate, grad_pre, ROWS_ROWS, preferred_element_type=f32
    ).astype(grads.dtype)
    summed = jnp.sum(grad_pre.astype(f32), axis=0, keepdims=True)
    parts = grads.shape[0]
    depth = 2 * width // parts
    tail = grads.shape[1] - depth
    bias_rows = jnp.broadcast_to(summed, (tail, width)).astype(grads.dtype)
    for part in range(parts):
        source, place = (
            (grad_self, part) if 2 * part < parts else (grad_neighbor, part - parts // 2)
        )
        grads[part, 0:depth, :] = source[place * depth : (place + 1) * depth, :]
        grads[part, depth:, :] = bias_rows


def layer(parts, features, mine, other, weight_self, weight_neighbor, bias, cotangent):
    row_total, width = features.shape
    shape = jax.ShapeDtypeStruct
    return pl.pallas_call(
        layer_kernel,
        out_shape=(
            shape((row_total, width), jnp.bfloat16),
            shape((width, row_total), jnp.bfloat16),
            shape((width, row_total), jnp.float32),
            shape((parts, 2 * width // parts + 16, width), jnp.bfloat16),
        ),
        name="layer",
    )(features, mine, other, weight_self, weight_neighbor, bias, cotangent)


def backward_kernel(
    cycle, replicas, pieces, sent_t, dense, grads, out, part_out,
    landed, held, part_landed, part_held, blocks, term,
    block_sem, send_sem, recv_sem,
):
    steps = blocks.shape[0]
    width = sent_t.shape[0]
    size = width // pieces
    f32 = jnp.float32
    group, replica, reverse, behind, ahead = ring_place(cycle, replicas)

    def load(step):
        return pltpu.make_async_copy(
            dense.at[step], blocks.at[step], block_sem.at[step]
        )

    def in_order(hop):
        return (steps - 1 - hop) * (1 - reverse) + hop * reverse

    @pl.loop(0, steps)
    def _(hop):
        load(in_order(hop)).start()

    greet((ahead, behind))

    def hop_copy(hop, piece):
        if piece < pieces:
            span = pl.ds(piece * size, size)
            source, target = held.at[hop, span], landed.at[hop, span]
        else:
            source, target = part_held.at[hop], part_landed.at[hop]
        return pltpu.make_async_remote_copy(
            src_ref=source,
            dst_ref=target,
            send_sem=send_sem.at[hop, piece],
            recv_sem=recv_sem.at[hop, piece],
            device_id={"blk": ahead},
            device_id_type=pl.DeviceIdType.MESH,
        )

    hops = steps - 1 + reverse

    @pl.loop(0, steps)
    def _(hop):
        step = in_order(hop)
        target = lax.rem(group - steps * replica - step + 2 * cycle, cycle)
        load(step).wait()
        term[...] = jnp.dot(sent_t[...], blocks[step], preferred_element_type=f32)
        for piece in range(pieces + 1):
            span = pl.ds(piece * size, size)

            @pl.when(hop > 0)
            def _():
                hop_copy(hop - 1, piece).wait_recv()
                if piece < pieces:
                    held[hop, span] = (
                        term[span] + landed[hop - 1, span].astype(f32)
                    ).astype(held.dtype)
                else:
                    part_held[hop] = (
                        grads[target].astype(f32) + part_landed[hop - 1].astype(f32)
                    ).astype(part_held.dtype)

            @pl.when(hop == 0)
            def _():
                if piece < pieces:
                    held[hop, span] = term[span].astype(held.dtype)
                else:
                    part_held[hop] = grads[target]

            @pl.when(hop < hops)
            def _():
                hop_copy(hop, piece).start()

    @pl.when(reverse == 0)
    def _():
        out[...] = held[steps - 1]
        part_out[...] = part_held[steps - 1]

    @pl.when(reverse == 1)
    def _():
        for piece in range(pieces + 1):
            hop_copy(steps - 1, piece).wait_recv()
        out[...] = landed[steps - 1]
        part_out[...] = part_landed[steps - 1]

    @pl.loop(0, hops)
    def _(hop):
        for piece in range(pieces + 1):
            hop_copy(hop, piece).wait_send()


def backward(cycle, replicas, sent_t, dense, grads):
    step_count, row_total, _ = dense.shape
    width = sent_t.shape[0]
    part = grads.shape[1:]
    pieces = 4
    bf16 = jnp.bfloat16
    return pl.pallas_call(
        functools.partial(backward_kernel, cycle, replicas, pieces),
        in_specs=[
            pl.BlockSpec(memory_space=pltpu.VMEM),
            pl.BlockSpec(memory_space=pl.ANY),
            pl.BlockSpec(memory_space=pltpu.VMEM),
        ],
        out_specs=[pl.BlockSpec(memory_space=pltpu.VMEM)] * 2,
        out_shape=(
            jax.ShapeDtypeStruct((width, row_total), bf16),
            jax.ShapeDtypeStruct(part, bf16),
        ),
        scratch_shapes=[
            pltpu.VMEM((step_count, width, row_total), bf16),
            pltpu.VMEM((step_count, width, row_total), bf16),
            pltpu.VMEM((step_count, *part), bf16),
            pltpu.VMEM((step_count, *part), bf16),
            pltpu.VMEM(dense.shape, bf16),
            pltpu.VMEM((width, row_total), jnp.float32),
            pltpu.SemaphoreType.DMA((step_count,)),
            pltpu.SemaphoreType.DMA((step_count, pieces + 1)),
            pltpu.SemaphoreType.DMA((step_count, pieces + 1)),
        ],
        compiler_params=pltpu.CompilerParams(collective_id=1, has_side_effects=True),
        name="backward",
    )(sent_t, dense, grads)


def spread_kernel(cycle, part, out, gathered, own_sem, send_sem, recv_sem):
    group = lax.axis_index("blk")
    greet([lax.rem(group + away, cycle) for away in range(1, cycle)])
    own = pltpu.make_async_copy(part, gathered.at[group], own_sem)
    own.start()

    def put(away):
        return pltpu.make_async_remote_copy(
            src_ref=part,
            dst_ref=gathered.at[group],
            send_sem=send_sem.at[away],
            recv_sem=recv_sem.at[away],
            device_id={"blk": lax.rem(group + away, cycle)},
            device_id_type=pl.DeviceIdType.MESH,
        )

    @pl.loop(1, cycle)
    def _(away):
        put(away).start()

    own.wait()

    @pl.loop(1, cycle)
    def _(away):
        put(away).wait()

    out[...] = gathered[...].astype(out.dtype)


def spread(cycle, part):
    return pl.pallas_call(
        functools.partial(spread_kernel, cycle),
        in_specs=[pl.BlockSpec(memory_space=pltpu.VMEM)],
        out_specs=pl.BlockSpec(memory_space=pltpu.VMEM),
        out_shape=jax.ShapeDtypeStruct((cycle, *part.shape), jnp.float32),
        scratch_shapes=[
            pltpu.VMEM((cycle, *part.shape), part.dtype),
            pltpu.SemaphoreType.DMA,
            pltpu.SemaphoreType.DMA((cycle,)),
            pltpu.SemaphoreType.DMA((cycle,)),
        ],
        compiler_params=pltpu.CompilerParams(collective_id=2, has_side_effects=True),
        name="spread",
    )(part)


def on_device(
    features,
    weight_self,
    weight_neighbor,
    bias_vector,
    tile_row,
    tile_column,
    tile_value,
    tile_count,
    tile_table,
    cotangent,
):
    f32, bf16 = jnp.float32, jnp.bfloat16
    cycle_length = lax.axis_size("blk")
    replicas = lax.axis_size("rep")
    step_count = cycle_length // replicas
    replica = lax.axis_index("rep")
    row_total, width = features.shape

    jump = jnp.minimum(replica, replicas - 1 - replica)
    jump_bits = max(replicas // 2 - 1, 0).bit_length()
    reverse = (2 * replica) // replicas

    def shifted(array, sign):
        for bit in range(jump_bits):
            by = sign * (step_count << bit)
            moved = jnp.where(
                reverse == 0,
                lax.ppermute(
                    array, "blk",
                    [(i, (i + by) % cycle_length) for i in range(cycle_length)],
                ),
                lax.ppermute(
                    array, "blk",
                    [(i, (i - by) % cycle_length) for i in range(cycle_length)],
                ),
            )
            array = jnp.where(jump // (1 << bit) % 2 == 1, moved, array)
        return array

    dense = build_dense(
        tile_row[0], tile_column[0], tile_value[0], tile_count[0], tile_table, row_total
    )
    mine = forward(cycle_length, replicas, shifted(features, 1), dense)
    bit = 1
    while True:
        other = lax.ppermute(mine, "rep", [(i, i ^ bit) for i in range(replicas)])
        bit *= 2
        if bit >= replicas:
            break
        mine = (mine.astype(f32) + other.astype(f32)).astype(bf16)
    activations, sent_t, self_t, grads = layer(
        cycle_length, features, mine, other, weight_self, weight_neighbor,
        bias_vector.reshape(1, width), cotangent,
    )
    pushed, part = backward(cycle_length, replicas, sent_t, dense, grads)
    pushed, part = shifted(pushed, -1), shifted(part, -1)

    def over_replicas(array):
        bit = 1
        while bit < replicas:
            other = lax.ppermute(array, "rep", [(i, i ^ bit) for i in range(replicas)])
            array = array.astype(f32) + other.astype(f32)
            bit *= 2
            if bit < replicas:
                array = array.astype(bf16)
        return array

    part = over_replicas(part)
    depth = 2 * width // cycle_length
    weights = spread(cycle_length, part[:depth].astype(bf16))
    weights = weights.reshape(2 * width, width)
    pushed = over_replicas(pushed)
    grad_features = (self_t + pushed).astype(bf16).T
    return (
        activations,
        grad_features,
        weights[:width],
        weights[width:],
        part[depth].astype(f32),
    )


def solution(mesh):
    placed = (
        P("blk", None),
        P(),
        P(),
        P(),
        P("blk", "rep", None),
        P("blk", "rep", None),
        P("blk", "rep", None),
        P("blk", "rep"),
        P(("blk", "rep"), None, None),
        P("blk", None),
    )
    return jax.shard_map(
        on_device,
        mesh=mesh,
        in_specs=placed,
        out_specs=(P("blk", None), P("blk", None), P(), P(), P()),
        check_vma=False,
    )
```

time: 343 us -> 168 us (0.49)
  waiting for transfers between devices: 273 us -> 19.8 us
  Pallas kernels: 46 us -> 125 us
  between operations: 13.8 us -> 0.67 us
  starting transfers between devices: 3.07 us -> 15.4 us
    reduce_scatter x1 -> x0, waiting for transfers between devices: 102 us -> none  [on_device(): pushed = lax.psum_scatter(partial, 'blk', scatter_dimension=0)]
    psum x1 -> x0, waiting for transfers between devices: 92 us -> none  [on_device(): grads = lax.psum(grads, 'blk').astype(f32)]
    pallas_call x2 -> x3, Pallas kernels: 28.8 us -> 108 us  [the longest x1 49.5 us: forward(): pl.pallas_call(functools.partial(forward_kernel, cycle, replicas, pieces)...]
    all_gather x1 -> x0, waiting for transfers between devices: 65.7 us -> none  [on_device(): panels = lax.all_gather(features, 'blk')]
    ppermute x1 -> x2, starting transfers between devices: 1.49 us -> 10.6 us  [over_replicas(): other = lax.ppermute(array, 'rep', [(i, i ^ bit) for i in range(replicas)])]
    ppermute x1 -> x2, waiting for transfers between devices: 0.01 us -> 8.07 us  [over_replicas(): other = lax.ppermute(array, 'rep', [(i, i ^ bit) for i in range(replicas)])]
  transfers between devices with their start and end apart: 5 -> 3, of which waited for: 4 -> 2; matrix products, arithmetic and copies ran while one was open for 1% -> 2% of each run, Pallas kernels for 4% -> 6%
where the time goes in v2:
time: 168 us
  Pallas kernels  125 us (74%)
  waiting for transfers between devices  19.8 us (12%)
  starting transfers between devices  15.4 us (9%)
  local copies, waits for them, and re-layouts  4.84 us (3%)
  other arithmetic  2.02 us (1%)
    pallas_call x1, Pallas kernels, forward(): pl.pallas_call(functools.partial(forward_kernel, cycle, replicas, pieces)...  49.5 us
    pallas_call x1, Pallas kernels, backward(): pl.pallas_call(functools.partial(backward_kernel, cycle, replicas, pieces...  47.7 us
    pallas_call x1, Pallas kernels, build_dense(): pl.pallas_call(build_kernel, grid_spec=pltpu.PrefetchScalarGridSpec(num_s...  12.8 us
    ppermute x1, waiting for transfers between devices, on_device(): other = lax.ppermute(mine, 'rep', [(i, i ^ bit) for i in range(replicas)])  11.7 us
    pallas_call x1, Pallas kernels, spread(): pl.pallas_call(functools.partial(spread_kernel, cycle), in_specs=[pl.Bloc...  10.8 us
    ppermute x2, starting transfers between devices, over_replicas(): other = lax.ppermute(array, 'rep', [(i, i ^ bit) for i in range(replicas)])  10.6 us
    ppermute x2, waiting for transfers between devices, over_replicas(): other = lax.ppermute(array, 'rep', [(i, i ^ bit) for i in range(replicas)])  8.07 us
    ppermute x1, starting transfers between devices, on_device(): other = lax.ppermute(mine, 'rep', [(i, i ^ bit) for i in range(replicas)])  4.82 us
  transfers between devices with their start and end apart: 3, of which 2 were waited for; matrix products, arithmetic and copies ran while one was open for 2% of the time, Pallas kernels for 6%

profile of v2, /device:TPU:0, one launch (start us, length us, event | category | flops | bytes accessed | tf_op | source)
XLA Modules:
  0.0 167.7 jit_solution(6173172774323242790)
XLA Ops:
  0.6 12.8 %build.1.dense = bf16[8,1024,1024]{2,1,0:T(8,128)(2,1)} custom-call(s32[8,64]{1,0:T(8,128)} %bitcast.12, s32[8,64]{1,0:T(8,128)} %bitcast.13, s32[8,64]{1,0:T(8,128)} %bitcast.14, s32[8]{0:T(128)} %bitcast.17, bf16[128,128,128]{2,1,0:T(8,128)(2,1)} %table.1), custom_call_target="tpu_custom_call" | custom-call | bytes 20971520 | tf_op jit(solution)/shard_map/build/pallas_call | solution.py:31
  13.4 49.5 %forward.1.mine = bf16[1024,256]{1,0:T(8,128)(2,1)} custom-call(bf16[1024,256]{1,0:T(8,128)(2,1)} %features.3, bf16[8,1024,1024]{2,1,0:T(8,128)(2,1)} %build.1.dense), custom_call_target="tpu_custom_call" | custom-call | tf_op jit(solution)/shard_map/forward/pallas_call | solution.py:137
  62.9 4.8 %collective-permute-start = (bf16[1024,256]{1,0:T(8,128)(2,1)}, bf16[1024,256]{1,0:T(8,128)(2,1)S(1)}, u32[]{:S(2)}, u32[]{:S(2)}) collective-permute-start(bf16[1024,256]{1,0:T(8,128)(2,1)} %forward.1.mine), channel_id=1, source_target_pairs={{0,1},{1,0},{2,3},{3,2},{4,5},{5,4},{6,7},{7,6},{8,9},{9,8},{10,11... | collective-permute-start | bytes 1572872 | tf_op jit(solution)/shard_map/ppermute | solution.py:430
  67.7 11.7 %collective-permute-done.other = bf16[1024,256]{1,0:T(8,128)(2,1)S(1)} collective-permute-done((bf16[1024,256]{1,0:T(8,128)(2,1)}, bf16[1024,256]{1,0:T(8,128)(2,1)S(1)}, u32[]{:S(2)}, u32[]{:S(2)}) %collective-permute-start) | collective-permute-done | bytes 524320 | tf_op jit(solution)/shard_map/ppermute | solution.py:430
  79.5 0.0 copy-start.1
  79.5 0.8 copy-done.1
  80.3 4.1 %layer.1 = (bf16[1024,256]{1,0:T(8,128)(2,1)}, bf16[256,1024]{1,0:T(8,128)(2,1)}, f32[256,1024]{1,0:T(8,128)}, bf16[16,48,256]{2,1,0:T(8,128)(2,1)}) custom-call(bf16[1024,256]{1,0:T(8,128)(2,1)} %features.3, bf16[1024,256]{1,0:T(8,128)(2,1)} %forward.1.mine, bf16[1024,256]{1,0:T(8,128)(2,1)} %copy-done.1, bf16[256,256]{1,0:T(8,128)(2,1)} %weight_self.1, ...), custom_call_target="tpu_custom_call" | custom-call | tf_op jit(solution)/shard_map/layer/pallas_call | solution.py:200
  84.4 0.0 copy-start
  84.4 47.7 %backward.1 = (bf16[256,1024]{1,0:T(8,128)(2,1)}, bf16[48,256]{1,0:T(8,128)(2,1)}) custom-call(bf16[256,1024]{1,0:T(8,128)(2,1)} %get-tuple-element.13.sent_t, bf16[8,1024,1024]{2,1,0:T(8,128)(2,1)} %build.1.dense, bf16[16,48,256]{2,1,0:T(8,128)(2,1)} %get-tuple-element.14.grads), custom_call_target="tpu_custom_call" | custom-call | tf_op jit(solution)/shard_map/backward/pallas_call | solution.py:310
  132.1 10.6 %collective-permute-start.1 = (bf16[256,1024]{1,0:T(8,128)(2,1)}, bf16[256,1024]{1,0:T(8,128)(2,1)S(1)}, u32[]{:S(2)}, u32[]{:S(2)}) collective-permute-start(bf16[256,1024]{1,0:T(8,128)(2,1)} %get-tuple-element.15), channel_id=1, source_target_pairs={{0,1},{1,0},{2,3},{3,2},{4,5},{5,4},{6,7},{7,6},{8,9},{9,8},{10,11... | collective-permute-start | bytes 1572872 | tf_op jit(solution)/shard_map/ppermute | solution.py:445
  142.6 0.1 collective-permute-start.2
  142.7 8.1 %collective-permute-done.2 = bf16[48,256]{1,0:T(8,128)(2,1)S(1)} collective-permute-done((bf16[48,256]{1,0:T(8,128)(2,1)}, bf16[48,256]{1,0:T(8,128)(2,1)S(1)}, u32[]{:S(2)}, u32[]{:S(2)}) %collective-permute-start.2) | collective-permute-done | bytes 24608 | tf_op jit(solution)/shard_map/ppermute | solution.py:445
  150.8 0.7 convert_add_fusion
  151.5 0.6 slice.26
  152.1 0.6 slice.28.part
  152.7 10.8 %spread.1 = f32[16,32,256]{2,1,0:T(8,128)} custom-call(bf16[32,256]{1,0:T(8,128)(2,1)} %slice.28.part), custom_call_target="tpu_custom_call" | custom-call | tf_op jit(solution)/shard_map/spread/pallas_call | solution.py:368
  163.5 1.9 %fusion.1 = (f32[8,32,256]{2,1,0:T(8,128)}, f32[8,32,256]{2,1,0:T(8,128)}) fusion(f32[16,32,256]{2,1,0:T(8,128)} %spread.1), kind=kLoop, calls=%fused_computation.4 | loop fusion | bytes 1048576 | tf_op jit(solution)/shard_map/slice | solution.py:462
  165.4 0.0 collective-permute-done.1
  165.4 0.0 copy-done
  165.4 1.3 fusion
  166.7 1.0 copy.15
Async XLA Ops:
  62.9 16.6 %collective-permute-start = (bf16[1024,256]{1,0:T(8,128)(2,1)}, bf16[1024,256]{1,0:T(8,128)(2,1)S(1)}, u32[]{:S(2)}, u32[]{:S(2)}) collective-permute-start(bf16[1024,256]{1,0:T(8,128)(2,1)} %forward.1.mine), channel_id=1, source_target_pairs={{0,1},{1,0},{2,3},{3,2},{4,5},{5,4},{6,7},{7,6},{8,9},{9,8},{10,11... | collective-permute-start | bytes 1572872 | tf_op jit(solution)/shard_map/ppermute | solution.py:430
  79.5 0.8 copy-start.1
  84.4 81.0 %copy-start = (f32[256,1024]{1,0:T(8,128)S(1)}, f32[256,1024]{1,0:T(8,128)}, u32[]{:S(2)}) copy-start(f32[256,1024]{1,0:T(8,128)} %get-tuple-element.12) | copy-start | bytes 3145732
  132.1 33.3 %collective-permute-start.1 = (bf16[256,1024]{1,0:T(8,128)(2,1)}, bf16[256,1024]{1,0:T(8,128)(2,1)S(1)}, u32[]{:S(2)}, u32[]{:S(2)}) collective-permute-start(bf16[256,1024]{1,0:T(8,128)(2,1)} %get-tuple-element.15), channel_id=1, source_target_pairs={{0,1},{1,0},{2,3},{3,2},{4,5},{5,4},{6,7},{7,6},{8,9},{9,8},{10,11... | collective-permute-start | bytes 1572872 | tf_op jit(solution)/shard_map/ppermute | solution.py:445
  142.6 8.1 %collective-permute-start.2 = (bf16[48,256]{1,0:T(8,128)(2,1)}, bf16[48,256]{1,0:T(8,128)(2,1)S(1)}, u32[]{:S(2)}, u32[]{:S(2)}) collective-permute-start(bf16[48,256]{1,0:T(8,128)(2,1)} %get-tuple-element.16), channel_id=1, source_target_pairs={{0,1},{1,0},{2,3},{3,2},{4,5},{5,4},{6,7},{7,6},{8,9},{9,8},{10,11... | collective-permute-start | bytes 73736 | tf_op jit(solution)/shard_map/ppermute | solution.py:445

commit v3 on v2

--- a/solution.py
+++ b/solution.py
@@ -130,23 +130,164 @@
             hop_copy(hop, piece).wait_send()
 
 
+LANES = 4
+OVER_LAYERS, OVER_PAIR, OVER_CORE, RELAYED = range(4)
+
+
+def layered_forward_kernel(
+    cycle, replicas, pieces, features, dense, out,
+    slots, blocks, total, block_sem, first_sem, send_sem, recv_sem,
+):
+    steps, rows = blocks.shape[0], blocks.shape[1]
+    group, _, reverse, _, _ = ring_place(cycle, replicas)
+    size = rows // pieces
+    layer_id, lane = group // LANES, lax.rem(group, LANES)
+    pair, core = lane // 2, lax.rem(lane, 2)
+    along = LANES * (1 - 2 * reverse)
+    ahead = lax.rem(group + along + cycle, cycle)
+    behind = lax.rem(group - along + cycle, cycle)
+    across = layer_id * LANES + (1 - pair) * 2 + core
+    beside = layer_id * LANES + pair * 2 + 1 - core
+    lane_across = (1 - pair) * 2 + core
+    first = pltpu.make_async_copy(features, slots.at[0, lane], first_sem)
+    first.start()
+
+    def load(step):
+        return pltpu.make_async_copy(
+            dense.at[step], blocks.at[step], block_sem.at[step]
+        )
+
+    def in_order(hop):
+        return hop * (1 - reverse) + (steps - 1 - hop) * reverse
+
+    @pl.loop(0, steps)
+    def _(hop):
+        load(in_order(hop)).start()
+
+    greet((ahead, behind, across, beside))
+    first.wait()
+
+    def copy(kind, distance, piece):
+        span = pl.ds(piece * size, size)
+        whose = lane_across if kind == RELAYED else lane
+        landing = distance + 1 if kind == OVER_LAYERS else distance
+        return pltpu.make_async_remote_copy(
+            src_ref=slots.at[distance, whose, span],
+            dst_ref=slots.at[landing, whose, span],
+            send_sem=send_sem.at[kind, distance, piece],
+            recv_sem=recv_sem.at[kind, distance, piece],
+            device_id={"blk": {OVER_LAYERS: ahead, OVER_PAIR: across}.get(kind, beside)},
+            device_id_type=pl.DeviceIdType.MESH,
+        )
+
+    def gives(distance):
+        return {0: pair == reverse, 1: None, 2: pair != reverse}[distance]
+
+    def gets(distance):
+        return {0: pair != reverse, 1: None, 2: pair == reverse}[distance]
+
+    def guarded(condition, act):
+        if condition is None:
+            act()
+        else:
+            pl.when(condition)(act)
+
+    def give(distance, piece):
+        if distance < 2:
+            copy(OVER_LAYERS, distance, piece).start()
+        guarded(gives(distance), lambda: copy(OVER_PAIR, distance, piece).start())
+        copy(OVER_CORE, distance, piece).start()
+
+    def relay(distance):
+        def act():
+            for piece in range(pieces):
+                copy(OVER_PAIR, distance, piece).wait_recv()
+                copy(RELAYED, distance, piece).start()
+
+        guarded(gets(distance), act)
+
+    def arrive(distance):
+        for piece in range(pieces):
+            copy(OVER_LAYERS, distance - 1, piece).wait_recv()
+            give(distance, piece)
+
+    def multiply(distance):
+        for piece in range(pieces):
+            copy(OVER_CORE, distance, piece).wait_recv()
+
+        def act():
+            for piece in range(pieces):
+                copy(RELAYED, distance, piece).wait_recv()
+
+        guarded(gets(distance), act)
+
+        @pl.loop(0, steps)
+        def _(hop):
+            step = in_order(hop)
+            away = hop + reverse
+            source = lax.rem(lane + (2 * reverse - 1) * away + 2 * steps, LANES)
+            far = ((LANES - 1 - lane) * (1 - reverse) + lane * reverse + away) // LANES
+
+            @pl.when(far == distance)
+            def _():
+                load(step).wait()
+                total[...] += jnp.dot(
+                    blocks[step], slots[distance, source],
+                    preferred_element_type=jnp.float32,
+                )
+
+    for piece in range(pieces):
+        give(0, piece)
+    total[...] = jnp.zeros_like(total)
+    arrive(1)
+    relay(0)
+    multiply(0)
+    relay(1)
+    arrive(2)
+    multiply(1)
+    relay(2)
+    multiply(2)
+    out[...] = total[...].astype(out.dtype)
+    for distance in range(3):
+        for piece in range(pieces):
+            if distance < 2:
+                copy(OVER_LAYERS, distance, piece).wait_send()
+            guarded(
+                gives(distance),
+                functools.partial(copy(OVER_PAIR, distance, piece).wait_send),
+            )
+            copy(OVER_CORE, distance, piece).wait_send()
+            guarded(
+                gets(distance),
+                functools.partial(copy(RELAYED, distance, piece).wait_send),
+            )
+
+
 def forward(cycle, replicas, features, dense):
     step_count, row_total, _ = dense.shape
     width = features.shape[1]
     pieces = 4
+    layered = step_count == 2 * LANES and cycle >= 3 * LANES and replicas == 2
+    if layered:
+        slots, sems = (3, LANES, row_total, width), (4, 3, pieces)
+    else:
+        slots, sems = (step_count + 1, row_total, width), (step_count, pieces)
     return pl.pallas_call(
-        functools.partial(forward_kernel, cycle, replicas, pieces),
+        functools.partial(
+            layered_forward_kernel if layered else forward_kernel,
+            cycle, replicas, pieces,
+        ),
         in_specs=[pl.BlockSpec(memory_space=pl.ANY)] * 2,
         out_specs=pl.BlockSpec(memory_space=pltpu.VMEM),
         out_shape=jax.ShapeDtypeStruct((row_total, width), jnp.bfloat16),
         scratch_shapes=[
-            pltpu.VMEM((step_count + 1, row_total, width), jnp.bfloat16),
+            pltpu.VMEM(slots, jnp.bfloat16),
             pltpu.VMEM(dense.shape, jnp.bfloat16),
             pltpu.VMEM((row_total, width), jnp.float32),
             pltpu.SemaphoreType.DMA((step_count,)),
             pltpu.SemaphoreType.DMA,
-            pltpu.SemaphoreType.DMA((step_count, pieces)),
-            pltpu.SemaphoreType.DMA((step_count, pieces)),
+            pltpu.SemaphoreType.DMA(sems),
+            pltpu.SemaphoreType.DMA(sems),
         ],
         compiler_params=pltpu.CompilerParams(collective_id=0, has_side_effects=True),
         name="forward",

time: 168 us -> 162 us (0.964)
  starting transfers between devices: 15.4 us -> 9.98 us
  Pallas kernels: 125 us -> 120 us
  waiting for transfers between devices: 19.8 us -> 23.5 us
    pallas_call x1, Pallas kernels: 49.5 us -> 44.6 us  [forward(): pl.pallas_call(functools.partial(layered_forward_kernel if layered else f...]
    ppermute x1, starting transfers between devices: 4.82 us -> 0.07 us  [on_device(): other = lax.ppermute(mine, 'rep', [(i, i ^ bit) for i in range(replicas)])]
    ppermute x1, waiting for transfers between devices: 11.7 us -> 14.6 us  [on_device(): other = lax.ppermute(mine, 'rep', [(i, i ^ bit) for i in range(replicas)])]
where the time goes in v3:
time: 162 us; the launch traced here: 161 us
  Pallas kernels  120 us (74%)
  waiting for transfers between devices  23.5 us (15%)
  starting transfers between devices  9.98 us (6%)
  local copies, waits for them, and re-layouts  4.84 us (3%)
  other arithmetic  2.02 us (1%)
    pallas_call x1, Pallas kernels, backward(): pl.pallas_call(functools.partial(backward_kernel, cycle, replicas, pieces...  47.7 us
    pallas_call x1, Pallas kernels, forward(): pl.pallas_call(functools.partial(layered_forward_kernel if layered else f...  44.6 us
    ppermute x1, waiting for transfers between devices, on_device(): other = lax.ppermute(mine, 'rep', [(i, i ^ bit) for i in range(replicas)])  14.6 us
    pallas_call x1, Pallas kernels, build_dense(): pl.pallas_call(build_kernel, grid_spec=pltpu.PrefetchScalarGridSpec(num_s...  13.1 us
    pallas_call x1, Pallas kernels, spread(): pl.pallas_call(functools.partial(spread_kernel, cycle), in_specs=[pl.Bloc...  10 us
    ppermute x2, starting transfers between devices, over_replicas(): other = lax.ppermute(array, 'rep', [(i, i ^ bit) for i in range(replicas)])  9.91 us
    ppermute x2, waiting for transfers between devices, over_replicas(): other = lax.ppermute(array, 'rep', [(i, i ^ bit) for i in range(replicas)])  8.87 us
    pallas_call x1, Pallas kernels, layer(): pl.pallas_call(layer_kernel, out_shape=(shape((row_total, width), jnp.bfl...  4.11 us
  transfers between devices with their start and end apart: 3, of which 2 were waited for; matrix products, arithmetic and copies ran while one was open for 2% of the time, Pallas kernels for 6%

profile of v3, /device:TPU:0, one launch (start us, length us, event | category | flops | bytes accessed | tf_op | source)
XLA Modules:
  0.0 160.7 jit_solution(9784933338526758770)
XLA Ops:
  0.6 13.1 %build.1.dense = bf16[8,1024,1024]{2,1,0:T(8,128)(2,1)} custom-call(s32[8,64]{1,0:T(8,128)} %bitcast.12, s32[8,64]{1,0:T(8,128)} %bitcast.13, s32[8,64]{1,0:T(8,128)} %bitcast.14, s32[8]{0:T(128)} %bitcast.17, bf16[128,128,128]{2,1,0:T(8,128)(2,1)} %table.1), custom_call_target="tpu_custom_call" | custom-call | bytes 20971520 | tf_op jit(solution)/shard_map/build/pallas_call | solution.py:31
  13.8 44.6 %forward.1.mine = bf16[1024,256]{1,0:T(8,128)(2,1)} custom-call(bf16[1024,256]{1,0:T(8,128)(2,1)} %features.3, bf16[8,1024,1024]{2,1,0:T(8,128)(2,1)} %build.1.dense), custom_call_target="tpu_custom_call" | custom-call | tf_op jit(solution)/shard_map/forward/pallas_call | solution.py:275
  58.4 0.1 collective-permute-start
  58.5 14.6 %collective-permute-done.other = bf16[1024,256]{1,0:T(8,128)(2,1)S(1)} collective-permute-done((bf16[1024,256]{1,0:T(8,128)(2,1)}, bf16[1024,256]{1,0:T(8,128)(2,1)S(1)}, u32[]{:S(2)}, u32[]{:S(2)}) %collective-permute-start) | collective-permute-done | bytes 524320 | tf_op jit(solution)/shard_map/ppermute | solution.py:571
  73.1 0.0 copy-start.1
  73.1 0.8 copy-done.1
  73.9 4.1 %layer.1 = (bf16[1024,256]{1,0:T(8,128)(2,1)}, bf16[256,1024]{1,0:T(8,128)(2,1)}, f32[256,1024]{1,0:T(8,128)}, bf16[16,48,256]{2,1,0:T(8,128)(2,1)}) custom-call(bf16[1024,256]{1,0:T(8,128)(2,1)} %features.3, bf16[1024,256]{1,0:T(8,128)(2,1)} %forward.1.mine, bf16[1024,256]{1,0:T(8,128)(2,1)} %copy-done.1, bf16[256,256]{1,0:T(8,128)(2,1)} %weight_self.1, ...), custom_call_target="tpu_custom_call" | custom-call | tf_op jit(solution)/shard_map/layer/pallas_call | solution.py:341
  78.0 0.0 copy-start
  78.0 47.7 %backward.1 = (bf16[256,1024]{1,0:T(8,128)(2,1)}, bf16[48,256]{1,0:T(8,128)(2,1)}) custom-call(bf16[256,1024]{1,0:T(8,128)(2,1)} %get-tuple-element.13.sent_t, bf16[8,1024,1024]{2,1,0:T(8,128)(2,1)} %build.1.dense, bf16[16,48,256]{2,1,0:T(8,128)(2,1)} %get-tuple-element.14.grads), custom_call_target="tpu_custom_call" | custom-call | tf_op jit(solution)/shard_map/backward/pallas_call | solution.py:451
  125.8 9.8 %collective-permute-start.1 = (bf16[256,1024]{1,0:T(8,128)(2,1)}, bf16[256,1024]{1,0:T(8,128)(2,1)S(1)}, u32[]{:S(2)}, u32[]{:S(2)}) collective-permute-start(bf16[256,1024]{1,0:T(8,128)(2,1)} %get-tuple-element.15), channel_id=1, source_target_pairs={{0,1},{1,0},{2,3},{3,2},{4,5},{5,4},{6,7},{7,6},{8,9},{9,8},{10,11... | collective-permute-start | bytes 1572872 | tf_op jit(solution)/shard_map/ppermute | solution.py:586
  135.6 0.1 collective-permute-start.2
  135.7 8.9 %collective-permute-done.2 = bf16[48,256]{1,0:T(8,128)(2,1)S(1)} collective-permute-done((bf16[48,256]{1,0:T(8,128)(2,1)}, bf16[48,256]{1,0:T(8,128)(2,1)S(1)}, u32[]{:S(2)}, u32[]{:S(2)}) %collective-permute-start.2) | collective-permute-done | bytes 24608 | tf_op jit(solution)/shard_map/ppermute | solution.py:586
  144.5 0.7 convert_add_fusion
  145.3 0.6 slice.26
  145.9 0.6 slice.28.part
  146.5 10.0 %spread.1 = f32[16,32,256]{2,1,0:T(8,128)} custom-call(bf16[32,256]{1,0:T(8,128)(2,1)} %slice.28.part), custom_call_target="tpu_custom_call" | custom-call | tf_op jit(solution)/shard_map/spread/pallas_call | solution.py:509
  156.5 1.9 %fusion.1 = (f32[8,32,256]{2,1,0:T(8,128)}, f32[8,32,256]{2,1,0:T(8,128)}) fusion(f32[16,32,256]{2,1,0:T(8,128)} %spread.1), kind=kLoop, calls=%fused_computation.4 | loop fusion | bytes 1048576 | tf_op jit(solution)/shard_map/slice | solution.py:603
  158.4 0.0 collective-permute-done.1
  158.4 0.0 copy-done
  158.4 1.3 fusion
  159.7 1.0 copy.15
Async XLA Ops:
  58.4 14.7 %collective-permute-start = (bf16[1024,256]{1,0:T(8,128)(2,1)}, bf16[1024,256]{1,0:T(8,128)(2,1)S(1)}, u32[]{:S(2)}, u32[]{:S(2)}) collective-permute-start(bf16[1024,256]{1,0:T(8,128)(2,1)} %forward.1.mine), channel_id=1, source_target_pairs={{0,1},{1,0},{2,3},{3,2},{4,5},{5,4},{6,7},{7,6},{8,9},{9,8},{10,11... | collective-permute-start | bytes 1572872 | tf_op jit(solution)/shard_map/ppermute | solution.py:571
  73.1 0.8 copy-start.1
  78.0 80.4 %copy-start = (f32[256,1024]{1,0:T(8,128)S(1)}, f32[256,1024]{1,0:T(8,128)}, u32[]{:S(2)}) copy-start(f32[256,1024]{1,0:T(8,128)} %get-tuple-element.12) | copy-start | bytes 3145732
  125.8 32.6 %collective-permute-start.1 = (bf16[256,1024]{1,0:T(8,128)(2,1)}, bf16[256,1024]{1,0:T(8,128)(2,1)S(1)}, u32[]{:S(2)}, u32[]{:S(2)}) collective-permute-start(bf16[256,1024]{1,0:T(8,128)(2,1)} %get-tuple-element.15), channel_id=1, source_target_pairs={{0,1},{1,0},{2,3},{3,2},{4,5},{5,4},{6,7},{7,6},{8,9},{9,8},{10,11... | collective-permute-start | bytes 1572872 | tf_op jit(solution)/shard_map/ppermute | solution.py:586
  135.6 8.9 %collective-permute-start.2 = (bf16[48,256]{1,0:T(8,128)(2,1)}, bf16[48,256]{1,0:T(8,128)(2,1)S(1)}, u32[]{:S(2)}, u32[]{:S(2)}) collective-permute-start(bf16[48,256]{1,0:T(8,128)(2,1)} %get-tuple-element.16), channel_id=1, source_target_pairs={{0,1},{1,0},{2,3},{3,2},{4,5},{5,4},{6,7},{7,6},{8,9},{9,8},{10,11... | collective-permute-start | bytes 73736 | tf_op jit(solution)/shard_map/ppermute | solution.py:586

commit v4 on v3

--- a/solution.py
+++ b/solution.py
@@ -476,50 +476,91 @@
     )(sent_t, dense, grads)
 
 
-def spread_kernel(cycle, part, out, gathered, own_sem, send_sem, recv_sem):
+def finish_kernel(
+    cycle, replicas, pushed, part, self_t, weights, bias_out, grad_t,
+    gathered, landed, part_landed, pair_send, pair_recv, send_sem, recv_sem,
+):
+    f32 = jnp.float32
+    depth = gathered.shape[1]
     group = lax.axis_index("blk")
-    greet([lax.rem(group + away, cycle) for away in range(1, cycle)])
-    own = pltpu.make_async_copy(part, gathered.at[group], own_sem)
-    own.start()
+    partner = {"rep": lax.rem(lax.axis_index("rep") + replicas // 2, replicas)}
+    mesh_id = pl.DeviceIdType.MESH
+    barrier = pltpu.get_barrier_semaphore()
+    pl.semaphore_signal(barrier, inc=1, device_id=partner, device_id_type=mesh_id)
+    for away in range(1, cycle):
+        pl.semaphore_signal(
+            barrier, inc=1, device_id={"blk": lax.rem(group + away, cycle)},
+            device_id_type=mesh_id,
+        )
+    pl.semaphore_wait(barrier, cycle)
+
+    def swap(source, target, index):
+        return pltpu.make_async_remote_copy(
+            src_ref=source, dst_ref=target,
+            send_sem=pair_send.at[index], recv_sem=pair_recv.at[index],
+            device_id=partner, device_id_type=mesh_id,
+        )
+
+    part_swap = swap(part, part_landed, 0)
+    part_swap.start()
+    panel_swap = swap(pushed, landed, 1)
+    panel_swap.start()
+    part_swap.wait()
+    summed = part[...].astype(f32) + part_landed[...].astype(f32)
+    bias_out[...] = summed[depth:]
+    gathered[group] = summed[:depth].astype(gathered.dtype)
 
     def put(away):
         return pltpu.make_async_remote_copy(
-            src_ref=part,
+            src_ref=gathered.at[group],
             dst_ref=gathered.at[group],
             send_sem=send_sem.at[away],
             recv_sem=recv_sem.at[away],
             device_id={"blk": lax.rem(group + away, cycle)},
-            device_id_type=pl.DeviceIdType.MESH,
+            device_id_type=mesh_id,
         )
 
     @pl.loop(1, cycle)
     def _(away):
         put(away).start()
 
-    own.wait()
-
     @pl.loop(1, cycle)
     def _(away):
         put(away).wait()
 
-    out[...] = gathered[...].astype(out.dtype)
-
-
-def spread(cycle, part):
+    weights[...] = gathered[...].astype(f32)
+    panel_swap.wait()
+    grad_t[...] = (
+        self_t[...] + (pushed[...].astype(f32) + landed[...].astype(f32))
+    ).astype(grad_t.dtype)
+
+
+def finish(cycle, replicas, pushed, part, self_t):
+    width = pushed.shape[0]
+    depth = 2 * width // cycle
+    tail = part.shape[0] - depth
+    shape = jax.ShapeDtypeStruct
     return pl.pallas_call(
-        functools.partial(spread_kernel, cycle),
-        in_specs=[pl.BlockSpec(memory_space=pltpu.VMEM)],
-        out_specs=pl.BlockSpec(memory_space=pltpu.VMEM),
-        out_shape=jax.ShapeDtypeStruct((cycle, *part.shape), jnp.float32),
+        functools.partial(finish_kernel, cycle, replicas),
+        in_specs=[pl.BlockSpec(memory_space=pltpu.VMEM)] * 3,
+        out_specs=[pl.BlockSpec(memory_space=pltpu.VMEM)] * 3,
+        out_shape=(
+            shape((cycle, depth, width), jnp.float32),
+            shape((tail, width), jnp.float32),
+            shape(pushed.shape, jnp.bfloat16),
+        ),
         scratch_shapes=[
-            pltpu.VMEM((cycle, *part.shape), part.dtype),
-            pltpu.SemaphoreType.DMA,
+            pltpu.VMEM((cycle, depth, width), jnp.bfloat16),
+            pltpu.VMEM(pushed.shape, jnp.bfloat16),
+            pltpu.VMEM(part.shape, jnp.bfloat16),
+            pltpu.SemaphoreType.DMA((2,)),
+            pltpu.SemaphoreType.DMA((2,)),
             pltpu.SemaphoreType.DMA((cycle,)),
             pltpu.SemaphoreType.DMA((cycle,)),
         ],
         compiler_params=pltpu.CompilerParams(collective_id=2, has_side_effects=True),
-        name="spread",
-    )(part)
+        name="finish",
+    )(pushed, part, self_t)
 
 
 def on_device(
@@ -582,26 +623,23 @@
 
     def over_replicas(array):
         bit = 1
-        while bit < replicas:
+        while 2 * bit < replicas:
             other = lax.ppermute(array, "rep", [(i, i ^ bit) for i in range(replicas)])
-            array = array.astype(f32) + other.astype(f32)
+            array = (array.astype(f32) + other.astype(f32)).astype(bf16)
             bit *= 2
-            if bit < replicas:
-                array = array.astype(bf16)
         return array
 
-    part = over_replicas(part)
-    depth = 2 * width // cycle_length
-    weights = spread(cycle_length, part[:depth].astype(bf16))
+    weights, bias_rows, grad_t = finish(
+        cycle_length, replicas, over_replicas(pushed), over_replicas(part), self_t
+    )
     weights = weights.reshape(2 * width, width)
-    pushed = over_replicas(pushed)
-    grad_features = (self_t + pushed).astype(bf16).T
+    grad_features = grad_t.T
     return (
         activations,
         grad_features,
         weights[:width],
         weights[width:],
-        part[depth].astype(f32),
+        bias_rows[0],
     )
 
 

time: 162 us -> 156 us (0.963)
  Pallas kernels: 120 us -> 135 us
  starting transfers between devices: 9.98 us -> 0.07 us
  waiting for transfers between devices: 23.5 us -> 14.6 us
  other arithmetic: 2.02 us -> 0 us
    pallas_call x1, Pallas kernels: 10 us -> 25.5 us  [finish(): pl.pallas_call(functools.partial(finish_kernel, cycle, replicas), in_spec...]
    ppermute x2 -> x0, starting transfers between devices: 9.91 us -> none  [over_replicas(): other = lax.ppermute(array, 'rep', [(i, i ^ bit) for i in range(replicas)])]
    ppermute x2 -> x0, waiting for transfers between devices: 8.87 us -> none  [over_replicas(): other = lax.ppermute(array, 'rep', [(i, i ^ bit) for i in range(replicas)])]
  transfers between devices with their start and end apart: 3 -> 1, of which waited for: 2 -> 1; matrix products, arithmetic and copies ran while one was open for 2% -> 0% of each run, Pallas kernels for 6% -> 0%
where the time goes in v4:
time: 156 us
  Pallas kernels  135 us (87%)
  waiting for transfers between devices  14.6 us (9%)
  local copies, waits for them, and re-layouts  5.96 us (4%)
    pallas_call x1, Pallas kernels, backward(): pl.pallas_call(functools.partial(backward_kernel, cycle, replicas, pieces...  47.3 us
    pallas_call x1, Pallas kernels, forward(): pl.pallas_call(functools.partial(layered_forward_kernel if layered else f...  44.8 us
    pallas_call x1, Pallas kernels, finish(): pl.pallas_call(functools.partial(finish_kernel, cycle, replicas), in_spec...  25.5 us
    ppermute x1, waiting for transfers between devices, on_device(): other = lax.ppermute(mine, 'rep', [(i, i ^ bit) for i in range(replicas)])  14.6 us
    pallas_call x1, Pallas kernels, build_dense(): pl.pallas_call(build_kernel, grid_spec=pltpu.PrefetchScalarGridSpec(num_s...  12.9 us
    pallas_call x1, Pallas kernels, layer(): pl.pallas_call(layer_kernel, out_shape=(shape((row_total, width), jnp.bfl...  4.1 us
  transfers between devices with their start and end apart: 1, of which 1 were waited for; matrix products, arithmetic and copies ran while one was open for 0% of the time, Pallas kernels for 0%

profile of v4, /device:TPU:0, one launch (start us, length us, event | category | flops | bytes accessed | tf_op | source)
XLA Modules:
  0.0 156.0 jit_solution(13273803055718157975)
XLA Ops:
  0.6 12.9 %build.1.dense = bf16[8,1024,1024]{2,1,0:T(8,128)(2,1)} custom-call(s32[8,64]{1,0:T(8,128)} %bitcast.12, s32[8,64]{1,0:T(8,128)} %bitcast.13, s32[8,64]{1,0:T(8,128)} %bitcast.14, s32[8]{0:T(128)} %bitcast.17, bf16[128,128,128]{2,1,0:T(8,128)(2,1)} %table.1), custom_call_target="tpu_custom_call" | custom-call | bytes 20971520 | tf_op jit(solution)/shard_map/build/pallas_call | solution.py:31
  13.5 44.8 %forward.1.mine = bf16[1024,256]{1,0:T(8,128)(2,1)} custom-call(bf16[1024,256]{1,0:T(8,128)(2,1)} %features.3, bf16[8,1024,1024]{2,1,0:T(8,128)(2,1)} %build.1.dense), custom_call_target="tpu_custom_call" | custom-call | tf_op jit(solution)/shard_map/forward/pallas_call | solution.py:275
  58.4 0.1 collective-permute-start
  58.5 14.6 %collective-permute-done.other = bf16[1024,256]{1,0:T(8,128)(2,1)S(1)} collective-permute-done((bf16[1024,256]{1,0:T(8,128)(2,1)}, bf16[1024,256]{1,0:T(8,128)(2,1)S(1)}, u32[]{:S(2)}, u32[]{:S(2)}) %collective-permute-start) | collective-permute-done | bytes 524320 | tf_op jit(solution)/shard_map/ppermute | solution.py:612
  73.1 0.0 copy-start
  73.1 0.8 copy-done
  73.9 4.1 %layer.1 = (bf16[1024,256]{1,0:T(8,128)(2,1)}, bf16[256,1024]{1,0:T(8,128)(2,1)}, f32[256,1024]{1,0:T(8,128)}, bf16[16,48,256]{2,1,0:T(8,128)(2,1)}) custom-call(bf16[1024,256]{1,0:T(8,128)(2,1)} %features.3, bf16[1024,256]{1,0:T(8,128)(2,1)} %forward.1.mine, bf16[1024,256]{1,0:T(8,128)(2,1)} %copy-done, bf16[256,256]{1,0:T(8,128)(2,1)} %weight_self.1, ...), custom_call_target="tpu_custom_call" | custom-call | tf_op jit(solution)/shard_map/layer/pallas_call | solution.py:341
  78.0 47.3 %backward.1 = (bf16[256,1024]{1,0:T(8,128)(2,1)}, bf16[48,256]{1,0:T(8,128)(2,1)}) custom-call(bf16[256,1024]{1,0:T(8,128)(2,1)} %get-tuple-element.15.sent_t, bf16[8,1024,1024]{2,1,0:T(8,128)(2,1)} %build.1.dense, bf16[16,48,256]{2,1,0:T(8,128)(2,1)} %get-tuple-element.16.grads), custom_call_target="tpu_custom_call" | custom-call | tf_op jit(solution)/shard_map/backward/pallas_call | solution.py:451
  125.3 25.5 %finish.1 = (f32[16,32,256]{2,1,0:T(8,128)}, f32[16,256]{1,0:T(8,128)}, bf16[256,1024]{1,0:T(8,128)(2,1)}) custom-call(bf16[256,1024]{1,0:T(8,128)(2,1)} %get-tuple-element.17.pushed, bf16[48,256]{1,0:T(8,128)(2,1)} %get-tuple-element.18.part, f32[256,1024]{1,0:T(8,128)} %get-tuple-element.19.self_t), custom_call_target="tpu_custom_call" | custom-call | tf_op jit(solution)/shard_map/finish/pallas_call | solution.py:543
  150.8 2.0 %copy.15 = bf16[1024,256]{1,0:T(8,128)(2,1)} copy(bf16[1024,256]{0,1:T(8,128)(2,1)} %bitcast.9) | data formatting | bytes 1048576
  152.9 1.3 slice.19
  154.1 1.9 %fusion = (f32[8,32,256]{2,1,0:T(8,128)}, f32[8,32,256]{2,1,0:T(8,128)}) fusion(f32[16,32,256]{2,1,0:T(8,128)} %get-tuple-element.21), kind=kLoop, calls=%fused_computation | loop fusion | bytes 1048576 | tf_op jit(solution)/shard_map/slice | solution.py:641
Async XLA Ops:
  58.4 14.7 %collective-permute-start = (bf16[1024,256]{1,0:T(8,128)(2,1)}, bf16[1024,256]{1,0:T(8,128)(2,1)S(1)}, u32[]{:S(2)}, u32[]{:S(2)}) collective-permute-start(bf16[1024,256]{1,0:T(8,128)(2,1)} %forward.1.mine), channel_id=1, source_target_pairs={{0,1},{1,0},{2,3},{3,2},{4,5},{5,4},{6,7},{7,6},{8,9},{9,8},{10,11... | collective-permute-start | bytes 1572872 | tf_op jit(solution)/shard_map/ppermute | solution.py:612
  73.1 0.8 copy-start
